TPU v7x, 32 devices: a whole 2x2x4 slice. The times are simulated.
32 devices in a mesh: row: 8 (over z, core), col: 4 (over y, x).
Axes of the slice: x: 2, y: 2, z: 4, core: 2. Of those that a mesh axis runs over, the one named last changes fastest.
Arguments:
- start_panel: bfloat16 [32768, 128], P(('col', 'row')), may hold values from -6 to 6
- block_values: bfloat16 [8, 4, 352, 128, 128], P('row', 'col'), may hold values from -0.078125 to 0.078125
- block_rows: int32 [8, 4, 352], P('row', 'col'), may hold values from 0 to 31, as said below
- block_cols: int32 [8, 4, 352], P('row', 'col'), may hold values from 0 to 63, as said below
- block_counts: int32 [8, 4], P('row', 'col'), may hold values from 141 to 352, as said below
Outputs:
- left_panel: bfloat16 [32768, 128], P(('row', 'col'))
- right_panel: bfloat16 [32768, 128], P(('col', 'row'))
Inputs may be any that keep to these rules, and one draw needn't show every extreme that they name: `block_rows`: block rows lie in 0 to 31 within each tile; low block rows hold more blocks; in every tile some live slot names block row 31. `block_cols`: in every tile some live slot names block column 63; a position may repeat. Only the first block_counts[r, c] slots of tile (r, c) are live; some tile fills all 352 slots.
All inputs are finite; a program needn't handle non-finite values.
Results may differ from a plain program's by a relative error of at most 0.0085.
Values may be sent and summed in bfloat16 or wider, within the bound.
No kernel may reach another device: no remote copies, remote signals or barrier semaphores. Data moves between devices by JAX's collectives and lax.ppermute only.
A program may use at most 128 MiB of HBM per device.

v0:
```python
import functools

import jax
import jax.numpy as jnp
from jax import lax
from jax.experimental import pallas as pl
from jax.experimental.pallas import tpu as pltpu
from jax.sharding import PartitionSpec as P


F32 = jnp.float32
BF16 = jnp.bfloat16
UNROLL = 32
STEP = 8
MARGIN = 4 * 1024 * 1024
VMEM = pl.BlockSpec(memory_space=pltpu.VMEM)
SMEM = pl.BlockSpec(memory_space=pltpu.SMEM)
ANY = pl.BlockSpec(memory_space=pl.ANY)
HBM = pl.BlockSpec(memory_space=pltpu.HBM)


def nbytes(item):
    total = jnp.dtype(item.dtype).itemsize
    for extent in item.shape:
        total *= extent
    return total


def params(items):
    return pltpu.CompilerParams(vmem_limit_bytes=sum(map(nbytes, items)) + MARGIN)


def swap(value, axis, mask):
    size = lax.axis_size(axis)
    return lax.ppermute(value, axis, [(i, i ^ mask) for i in range(size)])


def product_body(in_axis, forward, second, lists, values, shards, scratch, carried=None):
    in_me = lax.axis_index(in_axis)
    panel, acc, index, sems = scratch
    copies = [pltpu.make_async_copy(lists, index, sems.at[0])]
    for k, pieces in shards:
        length = sum(piece.shape[0] for piece in pieces)
        first = (in_me ^ k) * length
        for piece in pieces:
            place = panel.at[pl.ds(first, piece.shape[0])]
            copies.append(pltpu.make_async_copy(piece, place, sems.at[len(copies)]))
            first = first + piece.shape[0]
    for copy in copies:
        copy.start()
    acc[...] = jnp.zeros_like(acc) if carried is None else carried[...]
    for copy in copies:
        copy.wait()

    def one_group(g, carry):
        products = []
        targets = []
        for u in range(UNROLL):
            k = g * UNROLL + u
            block = values[index[0, k]]
            piece = panel[index[1, k]]
            if forward:
                products.append(jnp.dot(block, piece, preferred_element_type=F32))
            else:
                products.append(jnp.dot(piece, block, preferred_element_type=F32))
            targets.append(index[2, k])
        for target, product in zip(targets, products):
            acc[target] += product
        return carry

    low, high = (index[3, 0], index[4, 0]) if second else (0, index[3, 0])
    lax.fori_loop(low, high, one_group, 0)


def nested(form, refs):
    refs = iter(refs)
    return [[next(refs) for _ in range(pieces)] for pieces in form]


def halves(value):
    middle = value.shape[0] // 2
    return [value[:middle], value[middle:]] if middle else [value]


def block_of(pieces, b):
    for piece in pieces:
        if b < piece.shape[0]:
            return piece[b].astype(F32)
        b -= piece.shape[0]


def early_kernel(form, early, lists, values, *refs):
    shards, out, scratch = nested(form, refs), refs[sum(form)], refs[-4:]
    product_body("row", True, False, lists, values, list(zip(early, shards)), scratch)
    out[...] = scratch[1][...]


def left_kernel(form, late, lists, values, *refs):
    *shards, (carried,) = nested(form, refs)
    outs, scratch = refs[sum(form):-4], refs[-4:]
    product_body("row", True, True, lists, values, list(zip(late, shards)), scratch, carried)
    acc = scratch[1]
    per = (acc.shape[0] - 1) // len(outs)
    me = lax.axis_index("col")
    for k in range(len(outs)):
        part = acc[pl.ds((me ^ k) * per, per)]
        outs[k][...] = part.astype(outs[k].dtype)


def right_kernel(form, second, lists, values, *refs):
    shards, out, scratch = nested(form, refs), refs[sum(form)], refs[-4:]
    product_body("col", False, second, lists, values, list(enumerate(shards)), scratch)
    acc = scratch[1]
    per = out.shape[1]
    me = lax.axis_index("row")
    for k in range(out.shape[0]):
        distance = 2 * k + (0 if second else 1)
        out[k] = acc[pl.ds((me ^ distance) * per, per)].astype(out.dtype)


def run_product(kernel, other, lists, values, shards, panel_blocks, out_blocks, out_shape, carried=()):
    slots, size = values.shape[0], values.shape[-1]
    width = shards[0][0].shape[-1]
    shards = list(shards) + [[term] for term in carried]
    form = tuple(map(len, shards))
    shards = jax.tree.leaves(shards)
    held = [
        pltpu.VMEM((panel_blocks, size, width), BF16),
        pltpu.VMEM((out_blocks + 1, size, width), F32),
    ]
    return pl.pallas_call(
        functools.partial(kernel, form, other),
        out_shape=out_shape,
        in_specs=[ANY, VMEM] + [ANY] * (len(shards) - len(carried)) + [VMEM] * len(carried),
        out_specs=jax.tree.map(lambda _: VMEM, out_shape),
        scratch_shapes=held
        + [pltpu.SMEM(lists.shape, jnp.int32), pltpu.SemaphoreType.DMA((len(shards) + 1,))],
        compiler_params=params(held + jax.tree.leaves(out_shape) + [values] + list(carried)),
        cost_estimate=pl.CostEstimate(
            flops=2 * slots * size * size * width, bytes_accessed=2 * values.size, transcendentals=0
        ),
    )(lists, values, *shards)


def bucket_lists(second, target, source, live, spare, places):
    slots = target.shape[1]
    down = lax.broadcasted_iota(jnp.int32, (slots, slots), 0)
    along = lax.broadcasted_iota(jnp.int32, (slots, slots), 1)

    def column(values):
        return jnp.sum(jnp.where(down == along, values, 0.0), axis=1, keepdims=True)

    key = jnp.where(live, jnp.where(second, 1.0, 0.0), 2.0)
    before = jnp.sum(jnp.where((column(key) == key) & (down < along), 1.0, 0.0), axis=0, keepdims=True)
    steps = [
        jnp.floor((jnp.sum(jnp.where(key == bucket, 1.0, 0.0), axis=1, keepdims=True) + (UNROLL - 1.0)) / UNROLL)
        for bucket in (0.0, 1.0)
    ]
    place = column(jnp.where(live, before + key * steps[0] * UNROLL, -1.0))
    hit = lax.broadcasted_iota(jnp.int32, (slots, places), 1).astype(F32) == place
    number = lax.broadcasted_iota(jnp.int32, (slots, 1), 0).astype(F32)

    def placed(values, default):
        return jnp.sum(jnp.where(hit, values - default, 0.0), axis=0, keepdims=True) + default

    lists = [placed(number, 0.0), placed(column(source), 0.0), placed(column(target), spare)]
    return lists + [jnp.broadcast_to(count, (1, places)) for count in (steps[0], steps[0] + steps[1])]


def stage_kernel(row_blocks, col_blocks, per, counts, rows, cols, values, left, right, staged, sem):
    copy = pltpu.make_async_copy(values.at[0, 0], staged, sem)
    copy.start()
    row, col = rows[0], cols[0]
    live = lax.broadcasted_iota(jnp.int32, row.shape, 1) < counts[0, 0]
    row_size = col_blocks // per
    distance = lax.div(col, jnp.full_like(col, per)) ^ lax.axis_index("row")
    late = distance >= row_size - 2
    kept = (distance & 1) == 0
    row, col = row.astype(F32), col.astype(F32)
    places = left.shape[1]
    for out, lists in (
        (left, bucket_lists(late, row, col, live, float(row_blocks), places)),
        (right, bucket_lists(kept, col, row, live, float(col_blocks), places)),
    ):
        for k, line in enumerate(lists):
            out[k:k + 1, :] = line.astype(jnp.int32)
    copy.wait()


def left_sum_kernel(nodes_total, own, *refs):
    parts, (natural, flipped, gram) = refs[:-3], refs[-3:]
    total = jnp.zeros(gram.shape, F32)
    for b in range(own.shape[0]):
        summed = own[b]
        for part in parts:
            summed = summed + part[b].astype(F32)
        rounded = summed.astype(BF16)
        turned = summed.T.astype(BF16)
        natural[b] = rounded
        flipped[b] = turned
        total = total + jnp.dot(turned, rounded, preferred_element_type=F32)
    gram[...] = total / nodes_total


def core_sum_kernel(form, keep, came, *outs):
    for k, pieces in enumerate(nested(form, outs)):
        first = 0
        for out in pieces:
            span = pl.ds(first, out.shape[0])
            out[...] = (keep[k, span] + came[k, span].astype(F32)).astype(out.dtype)
            first += out.shape[0]


def inverse_lower(gram):
    order = gram.shape[0]
    panels = order // STEP
    lanes = lax.broadcasted_iota(jnp.int32, (STEP, order), 1)
    strips = [gram[t * STEP:(t + 1) * STEP, :] for t in range(panels)]
    finals = []

    def column(strip, lane):
        return jnp.broadcast_to(strip[:, lane:lane + 1], strip.shape)

    def row(strip, sub):
        return jnp.broadcast_to(strip[sub:sub + 1, :], strip.shape)

    for t in range(panels):
        base = t * STEP
        strip = strips[t]
        cols = [column(strip, base + s) for s in range(STEP)]
        scales, weights, rows_done = [], [], []
        for s in range(STEP):
            scale = lax.rsqrt(row(cols[s], s))
            lower = cols[s] * scale
            scales.append(scale)
            picks = [None] * STEP
            for u in range(s + 1, STEP):
                picks[u] = row(lower, u)
                cols[u] = cols[u] - lower * picks[u]
            weights.append(picks)
            done = jnp.where(lanes == base + s, scale, row(strip, s) * scale)
            done = jnp.where((lanes > base + s) & (lanes < base + STEP), 0.0, done)
            rows_done.append(done)
            if s + 1 < STEP:
                strip = jnp.where(lanes == base + s, 0.0, strip) - lower * done
        sub = lax.broadcasted_iota(jnp.int32, (STEP, order), 0)
        final = rows_done[0]
        for s in range(1, STEP):
            final = jnp.where(sub == s, rows_done[s], final)
        finals.append(jnp.where(lanes <= base + sub, final, 0.0))
        inside = (lanes >= base) & (lanes < base + STEP)
        for v in range(t + 1, panels):
            below = strips[v]
            parts = [column(below, base + s) for s in range(STEP)]
            update = jnp.where(inside, 0.0, below)
            for s in range(STEP):
                part = parts[s] * scales[s]
                for u in range(s + 1, STEP):
                    parts[u] = parts[u] - part * weights[s][u]
                update = update - part * rows_done[s]
            strips[v] = update
    return finals


def limbs(value, depth):
    terms = []
    for _ in range(depth):
        term = value.astype(BF16)
        value = value - term.astype(F32)
        terms.append(term)
    return terms


def fold(stacked, order):
    total = stacked[-order:]
    for low in range(stacked.shape[0] - 2 * order, -1, -order):
        total = stacked[low:low + order] + total
    return total


def factor_of(parts, scratch):
    total = parts[0][...]
    for part in parts[1:]:
        total = total + part[...].astype(F32)
    for t, strip in enumerate(inverse_lower(total)):
        scratch[t * STEP:(t + 1) * STEP, :] = strip
    return scratch[...]


def right_sum_kernel(form, nodes_total, inverse, own, *refs):
    parts, (flipped, gram) = nested(form, refs), refs[-2:]
    order = inverse.shape[0]
    factor = limbs(inverse[...], 3)
    full, head = jnp.concatenate(factor, 0), jnp.concatenate(factor[:2], 0)
    total = jnp.zeros(gram.shape, F32)
    for b in range(own.shape[0]):
        summed = own[b]
        for part in parts:
            summed = summed + block_of(part, b)
        first, second = limbs(summed, 2)
        scaled = fold(jnp.dot(head, second, preferred_element_type=F32), order)
        scaled = scaled + fold(jnp.dot(full, first, preferred_element_type=F32), order)
        rounded = scaled.astype(BF16)
        flipped[b] = rounded
        total = total + lax.dot_general(rounded, rounded, (((1,), (1,)), ((), ())), preferred_element_type=F32)
    gram[...] = total / nodes_total


def left_factor_kernel(*refs):
    parts, natural, inverse, out = refs[:-3], refs[-3], refs[-2], refs[-1]
    factor = factor_of(parts, inverse)
    terms = limbs(factor, 3)
    for b in range(natural.shape[0]):
        solved = jnp.zeros(out.shape[1:], F32)
        for term in reversed(terms):
            solved = solved + lax.dot_general(
                natural[b], term, (((1,), (1,)), ((), ())), preferred_element_type=F32
            )
        out[b] = solved.astype(BF16)


def right_factor_kernel(*refs):
    parts, flipped, out, scratch = refs[:-3], refs[-3], refs[-2], refs[-1]
    factor = factor_of(parts, scratch)
    stacked = jnp.concatenate(limbs(factor, 3), 0)
    for b in range(flipped.shape[0]):
        solved = fold(jnp.dot(stacked, flipped[b], preferred_element_type=F32), factor.shape[0])
        out[b] = solved.T.astype(BF16)


def call(kernel, out_shape, *args, scratch=()):
    return pl.pallas_call(
        kernel,
        out_shape=out_shape,
        in_specs=[VMEM] * len(args),
        out_specs=jax.tree.map(lambda _: VMEM, out_shape),
        scratch_shapes=scratch,
        compiler_params=params(list(args) + jax.tree.leaves(out_shape) + list(scratch)),
    )(*args)


def shape(dims, kind):
    return jax.ShapeDtypeStruct(dims, kind)


def exchange(value, axis, first, step=1):
    sent = value.astype(BF16)
    return [value] + [swap(sent, axis, k) for k in range(first, lax.axis_size(axis), step)]


def add_parts(parts):
    return functools.reduce(lambda total, part: total + part.astype(total.dtype), parts)


def gather_row(shard):
    row_size = lax.axis_size("row")
    top = row_size // 2
    have = {0: [shard], top: [swap(piece, "row", top) for piece in halves(shard)]}
    bit = top // 2
    while bit:
        for k in sorted(have, reverse=True):
            have[k | bit] = [swap(piece, "row", bit) for piece in have[k]]
        bit //= 2
    return [have[k] for k in range(row_size)]


def collect_row(terms):
    row_size = lax.axis_size("row")
    came = []
    bit = 2
    while bit < row_size:
        for k in sorted(terms, reverse=True):
            if not k & bit:
                continue
            moved = [swap(piece.astype(BF16), "row", bit) for piece in terms.pop(k)]
            if k ^ bit:
                terms[k ^ bit] = [(a + b.astype(F32)) for a, b in zip(terms[k ^ bit], moved)]
            else:
                came.append(moved)
        bit *= 2
    return came


def local(start_panel, block_values, block_rows, block_cols, block_counts):
    group_rows, width = start_panel.shape
    row_size = lax.axis_size("row")
    col_size = lax.axis_size("col")
    nodes_total = group_rows * row_size * col_size
    size = block_values.shape[-1]
    slots = block_values.shape[2]
    per = group_rows // size
    row_blocks, col_blocks = per * col_size, per * row_size
    block = (per, size, width)
    square = shape((width, width), F32)
    places = (-(-slots // UNROLL) + 2) * UNROLL
    staged = (shape((5, places), jnp.int32),) * 2 + (shape((slots, size, size), BF16),)
    left_list, right_list, values = pl.pallas_call(
        functools.partial(stage_kernel, row_blocks, col_blocks, per),
        out_shape=staged,
        in_specs=[SMEM, VMEM, VMEM, HBM],
        out_specs=(VMEM,) * len(staged),
        scratch_shapes=[pltpu.SemaphoreType.DMA(())],
        compiler_params=params(staged),
    )(block_counts, block_rows, block_cols, block_values)

    shards = gather_row(start_panel.reshape(block))
    early, late = range(row_size - 2), range(row_size - 2, row_size)
    carried = run_product(
        early_kernel, early, left_list, values, [shards[k] for k in early], col_blocks, row_blocks,
        shape((row_blocks + 1, size, width), F32),
    )
    parts = run_product(
        left_kernel, late, left_list, values, [shards[k] for k in late], col_blocks, row_blocks,
        [shape(block, F32)] + [shape(block, BF16)] * (col_size - 1), (carried,),
    )
    came = [swap(parts[k], "col", k) for k in range(1, col_size)]
    natural, flipped, gram = call(
        functools.partial(left_sum_kernel, nodes_total),
        (shape(block, BF16), shape(block, BF16), square), parts[0], *came,
    )
    turned = exchange(flipped, "col", 1)
    gram = add_parts(exchange(gram + swap(gram, "row", 1), "row", 2, 2))
    gram, turned = lax.optimization_barrier((gram, turned))

    half = (row_size // 2,) + block
    turned = [[part] for part in turned]
    send = run_product(
        right_kernel, False, right_list, values, turned, row_blocks, col_blocks, shape(half, BF16)
    )
    returned = swap(send, "row", 1)
    keep = run_product(
        right_kernel, True, right_list, values, turned, row_blocks, col_blocks, shape(half, F32)
    )
    pieces = {0: [shape(block, F32)]}
    for k in range(2, row_size, 2):
        far = 2 if k & (row_size // 2) and per % 2 == 0 else 1
        kind = BF16 if k & 2 else F32
        pieces[k] = [shape((per // far, size, width), kind)] * far
    form = tuple(map(len, pieces.values()))
    sums = call(
        functools.partial(core_sum_kernel, form), jax.tree.leaves(list(pieces.values())), keep, returned
    )
    terms = dict(zip(pieces, nested(form, sums)))
    (own,) = terms.pop(0)
    gram, _ = lax.optimization_barrier((gram, own))
    came = collect_row(terms)
    grams = exchange(gram, "col", 1)
    inverse, left_panel = call(left_factor_kernel, (square, shape(block, BF16)), *grams, natural)
    right_flipped, gram = call(
        functools.partial(right_sum_kernel, tuple(map(len, came)), nodes_total),
        (shape(block, BF16), square), inverse, own, *jax.tree.leaves(came),
    )
    gram = gram + swap(gram, "row", 1)
    gram = add_parts(exchange(gram, "col", 1))
    right_panel = call(
        right_factor_kernel, shape(block, BF16), *exchange(gram, "row", 2, 2), right_flipped,
        scratch=[pltpu.VMEM((width, width), F32)],
    )
    return (left_panel.reshape(group_rows, width), right_panel.reshape(group_rows, width))


def solution(mesh):
    return jax.shard_map(
        local,
        mesh=mesh,
        in_specs=(
            P(("col", "row"), None),
            P("row", "col", None, None, None),
            P("row", "col", None),
            P("row", "col", None),
            P("row", "col"),
        ),
        out_specs=(P(("row", "col"), None), P(("col", "row"), None)),
        check_vma=False,
    )
```

profile of v0, /device:TPU:0, one launch (start us, length us, event | category | flops | bytes accessed | tf_op | source)
XLA Modules:
  0.0 124.4 jit_solution(1706566417075118386)
XLA Ops:
  0.6 3.1 %collective-permute-start.7 = (bf16[8,128,128]{2,1,0:T(8,128)(2,1)}, bf16[8,128,128]{2,1,0:T(8,128)(2,1)S(1)}, u32[]{:S(2)}, u32[]{:S(2)}) collective-permute-start(bf16[8,128,128]{2,1,0:T(8,128)(2,1)} %bitcast.5), channel_id=1, source_target_pairs={{0,8},{4,12},{8,0},{12,4},{16,24},{20,28},{24,16},{28,20},{1,9},{5... | collective-permute-start | bytes 786440 | tf_op jit(solution)/shard_map/ppermute | solution.py:35
  3.8 1.0 fusion.3
  4.8 2.7 %collective-permute-start = (bf16[4,128,128]{2,1,0:T(8,128)(2,1)S(1)}, bf16[4,128,128]{2,1,0:T(8,128)(2,1)S(1)}, u32[]{:S(2)}, u32[]{:S(2)}) collective-permute-start(bf16[4,128,128]{2,1,0:T(8,128)(2,1)S(1)} %bitcast.10), channel_id=1, source_target_pairs={{0,16},{4,20},{8,24},{12,28},{16,0},{20,4},{24,8},{28,12},{1,17},{... | collective-permute-start | bytes 393224 | tf_op jit(solution)/shard_map/ppermute | solution.py:35
  7.4 0.3 collective-permute-start.2
  7.7 5.8 %collective-permute-done.refs_4_ = bf16[4,128,128]{2,1,0:T(8,128)(2,1)S(1)} collective-permute-done((bf16[4,128,128]{2,1,0:T(8,128)(2,1)S(1)}, bf16[4,128,128]{2,1,0:T(8,128)(2,1)S(1)}, u32[]{:S(2)}, u32[]{:S(2)}) %collective-permute-start) | collective-permute-done | bytes 131104 | tf_op jit(solution)/shard_map/ppermute | solution.py:35
  13.5 0.5 collective-permute-start.6
  14.0 0.9 collective-permute-done.7.refs_2_
  14.9 2.8 %collective-permute-start.1 = (bf16[4,128,128]{2,1,0:T(8,128)(2,1)S(1)}, bf16[4,128,128]{2,1,0:T(8,128)(2,1)S(1)}, u32[]{:S(2)}, u32[]{:S(2)}) collective-permute-start(bf16[4,128,128]{2,1,0:T(8,128)(2,1)S(1)} %collective-permute-done.refs_4_), channel_id=1, source_target_pairs={{0,8},{4,12},{8,0},{12,4},{16,24},{20,28},{24,16},{28,20},{1,9},{5... | collective-permute-start | bytes 393224 | tf_op jit(solution)/shard_map/ppermute | solution.py:35
  17.7 1.4 %collective-permute-done.2.refs_5_ = bf16[4,128,128]{2,1,0:T(8,128)(2,1)S(1)} collective-permute-done((bf16[4,128,128]{2,1,0:T(8,128)(2,1)S(1)}, bf16[4,128,128]{2,1,0:T(8,128)(2,1)S(1)}, u32[]{:S(2)}, u32[]{:S(2)}) %collective-permute-start.2) | collective-permute-done | bytes 131104 | tf_op jit(solution)/shard_map/ppermute | solution.py:35
  19.8 4.3 %copy-done = bf16[1,1,352,128,128]{4,3,2,1,0:T(8,128)(2,1)S(1)} copy-done((bf16[1,1,352,128,128]{4,3,2,1,0:T(8,128)(2,1)S(1)}, bf16[1,1,352,128,128]{4,3,2,1,0:T(8,128)(2,1)}, u32[]{:S(2)}) %copy-start) | copy-done | bytes 11534360
  24.1 0.7 copy-done.2
  24.8 0.7 copy-done.3
  25.5 1.5 %shard_map.68 = (s32[5,416]{1,0:T(8,128)S(1)}, s32[5,416]{1,0:T(8,128)S(1)}, bf16[352,128,128]{2,1,0:T(8,128)(2,1)S(1)}) custom-call(s32[1,1]{1,0:T(1,128)S(6)} %copy.7.counts, s32[1,1,352]{2,1,0:T(1,128)S(1)} %copy-done.2, s32[1,1,352]{2,1,0:T(1,128)S(1)} %copy-done.3, bf16[1,1,352,128,128]{4,3,2,1,0:T(8,128)(2,1)S(1)} %copy-done), custom_call_target="tpu_custom_call" | custom-call | tf_op jit(solution)/shard_map/pallas_call | solution.py:397
  27.0 0.6 collective-permute-start.4
  27.6 0.1 collective-permute-start.5
  27.7 3.0 %shard_map.69.refs_4_ = f32[33,128,128]{2,1,0:T(8,128)S(1)} custom-call(s32[5,416]{1,0:T(8,128)S(1)} %get-tuple-element.28.lists, bf16[352,128,128]{2,1,0:T(8,128)(2,1)S(1)} %get-tuple-element.29.values, bf16[8,128,128]{2,1,0:T(8,128)(2,1)S(1)} %bitcast.7, bf16[8,128,128]{2,1,0:T(8,128)(2,1)S(1)} %collective-permute-done.6.refs_1_, ...), custom_call_target="tpu_custom_call" | custom-call | flops 1476395008 | bytes 11534336 | tf_op jit(solution)/shard_map/pallas_call | solution.py:131
  30.8 2.0 %shard_map.70 = (f32[8,128,128]{2,1,0:T(8,128)S(1)}, bf16[8,128,128]{2,1,0:T(8,128)(2,1)S(1)}, bf16[8,128,128]{2,1,0:T(8,128)(2,1)S(1)}, bf16[8,128,128]{2,1,0:T(8,128)(2,1)S(1)}) custom-call(s32[5,416]{1,0:T(8,128)S(1)} %get-tuple-element.28.lists, bf16[352,128,128]{2,1,0:T(8,128)(2,1)S(1)} %get-tuple-element.29.values, ...), custom_call_target="tpu_custom_call" | custom-call | flops 1476395008 | bytes 11534336 | tf_op jit(solution)/shard_map/pallas_call | solution.py:131
  32.7 1.6 %collective-permute-start.11 = (bf16[8,128,128]{2,1,0:T(8,128)(2,1)S(1)}, bf16[8,128,128]{2,1,0:T(8,128)(2,1)S(1)}, u32[]{:S(2)}, u32[]{:S(2)}) collective-permute-start(bf16[8,128,128]{2,1,0:T(8,128)(2,1)S(1)} %get-tuple-element.31), channel_id=1, source_target_pairs={{0,1},{1,0},{2,3},{3,2},{4,5},{5,4},{6,7},{7,6},{8,9},{9,8},{10,11... | collective-permute-start | bytes 786440 | tf_op jit(solution)/shard_map/ppermute | solution.py:35
  34.3 2.0 %collective-permute-start.12 = (bf16[8,128,128]{2,1,0:T(8,128)(2,1)S(1)}, bf16[8,128,128]{2,1,0:T(8,128)(2,1)S(1)}, u32[]{:S(2)}, u32[]{:S(2)}) collective-permute-start(bf16[8,128,128]{2,1,0:T(8,128)(2,1)S(1)} %get-tuple-element.32), channel_id=1, source_target_pairs={{0,2},{1,3},{2,0},{3,1},{4,6},{5,7},{6,4},{7,5},{8,10},{9,11},{10,... | collective-permute-start | bytes 786440 | tf_op jit(solution)/shard_map/ppermute | solution.py:35
  36.3 1.4 %collective-permute-start.13 = (bf16[8,128,128]{2,1,0:T(8,128)(2,1)S(1)}, bf16[8,128,128]{2,1,0:T(8,128)(2,1)S(1)}, u32[]{:S(2)}, u32[]{:S(2)}) collective-permute-start(bf16[8,128,128]{2,1,0:T(8,128)(2,1)S(1)} %get-tuple-element.33), channel_id=1, source_target_pairs={{0,3},{1,2},{2,1},{3,0},{4,7},{5,6},{6,5},{7,4},{8,11},{9,10},{10,... | collective-permute-start | bytes 786440 | tf_op jit(solution)/shard_map/ppermute | solution.py:35
  37.7 2.7 %collective-permute-done.11.refs_0_ = bf16[8,128,128]{2,1,0:T(8,128)(2,1)S(1)} collective-permute-done((bf16[8,128,128]{2,1,0:T(8,128)(2,1)S(1)}, bf16[8,128,128]{2,1,0:T(8,128)(2,1)S(1)}, u32[]{:S(2)}, u32[]{:S(2)}) %collective-permute-start.11) | collective-permute-done | bytes 262176 | tf_op jit(solution)/shard_map/ppermute | solution.py:35
  40.4 7.6 %collective-permute-done.12.refs_1_ = bf16[8,128,128]{2,1,0:T(8,128)(2,1)S(1)} collective-permute-done((bf16[8,128,128]{2,1,0:T(8,128)(2,1)S(1)}, bf16[8,128,128]{2,1,0:T(8,128)(2,1)S(1)}, u32[]{:S(2)}, u32[]{:S(2)}) %collective-permute-start.12) | collective-permute-done | bytes 262176 | tf_op jit(solution)/shard_map/ppermute | solution.py:35
  48.0 1.6 %collective-permute-done.13.refs_2_ = bf16[8,128,128]{2,1,0:T(8,128)(2,1)S(1)} collective-permute-done((bf16[8,128,128]{2,1,0:T(8,128)(2,1)S(1)}, bf16[8,128,128]{2,1,0:T(8,128)(2,1)S(1)}, u32[]{:S(2)}, u32[]{:S(2)}) %collective-permute-start.13) | collective-permute-done | bytes 262176 | tf_op jit(solution)/shard_map/ppermute | solution.py:35
  49.6 0.3 shard_map.71
  50.0 1.2 collective-permute-done.14
  51.3 4.1 %collective-permute-start.17 = (bf16[128,128]{1,0:T(8,128)(2,1)S(1)}, bf16[128,128]{1,0:T(8,128)(2,1)S(1)}, u32[]{:S(2)}, u32[]{:S(2)}) collective-permute-start(bf16[128,128]{1,0:T(8,128)(2,1)S(1)} %get-tuple-element.58), channel_id=1, source_target_pairs={{0,24},{4,28},{8,16},{12,20},{16,8},{20,12},{24,0},{28,4},{1,25},{... | collective-permute-start | bytes 98312 | tf_op jit(solution)/shard_map/ppermute | solution.py:35
  55.5 0.6 collective-permute-start.15
  56.1 1.5 %collective-permute-start.20 = (bf16[8,128,128]{2,1,0:T(8,128)(2,1)S(1)}, bf16[8,128,128]{2,1,0:T(8,128)(2,1)S(1)}, u32[]{:S(2)}, u32[]{:S(2)}) collective-permute-start(bf16[8,128,128]{2,1,0:T(8,128)(2,1)S(1)} %get-tuple-element.38.refs_0_), channel_id=1, source_target_pairs={{0,3},{1,2},{2,1},{3,0},{4,7},{5,6},{6,5},{7,4},{8,11},{9,10},{10,... | collective-permute-start | bytes 786440 | tf_op jit(solution)/shard_map/ppermute | solution.py:35
  57.6 0.8 collective-permute-start.19
  58.4 1.2 collective-permute-start.18
  59.6 0.7 collective-permute-done.16
  60.3 5.9 %collective-permute-done.20.refs_3_ = bf16[8,128,128]{2,1,0:T(8,128)(2,1)S(1)} collective-permute-done((bf16[8,128,128]{2,1,0:T(8,128)(2,1)S(1)}, bf16[8,128,128]{2,1,0:T(8,128)(2,1)S(1)}, u32[]{:S(2)}, u32[]{:S(2)}) %collective-permute-start.20) | collective-permute-done | bytes 262176 | tf_op jit(solution)/shard_map/ppermute | solution.py:35
  66.2 4.2 %collective-permute-done.19.refs_2_ = bf16[8,128,128]{2,1,0:T(8,128)(2,1)S(1)} collective-permute-done((bf16[8,128,128]{2,1,0:T(8,128)(2,1)S(1)}, bf16[8,128,128]{2,1,0:T(8,128)(2,1)S(1)}, u32[]{:S(2)}, u32[]{:S(2)}) %collective-permute-start.19) | collective-permute-done | bytes 262176 | tf_op jit(solution)/shard_map/ppermute | solution.py:35
  70.4 2.4 %shard_map.73 = bf16[4,8,128,128]{3,2,1,0:T(8,128)(2,1)S(1)} custom-call(s32[5,416]{1,0:T(8,128)S(1)} %get-tuple-element.37.lists, bf16[352,128,128]{2,1,0:T(8,128)(2,1)S(1)} %get-tuple-element.29.values, bf16[8,128,128]{2,1,0:T(8,128)(2,1)S(1)} %get-tuple-element.38.refs_0_, bf16[8,128,128]{2,1,0:T(8,128)(2,1)S(1)} %collective-permute-done.18.refs_1_, ...), custom_call_target="tpu_custom_call" | custom-call | flops 1476395008 | bytes 11534336 | tf_op jit(solution)/shard_map/pallas_call | solution.py:131
  72.8 1.5 %collective-permute-start.21 = (bf16[4,8,128,128]{3,2,1,0:T(8,128)(2,1)S(1)}, bf16[4,8,128,128]{3,2,1,0:T(8,128)(2,1)S(1)}, u32[]{:S(2)}, u32[]{:S(2)}) collective-permute-start(bf16[4,8,128,128]{3,2,1,0:T(8,128)(2,1)S(1)} %shard_map.73), channel_id=1, source_target_pairs={{0,4},{4,0},{8,12},{12,8},{16,20},{20,16},{24,28},{28,24},{1,5},{5... | collective-permute-start | bytes 3145736 | tf_op jit(solution)/shard_map/ppermute | solution.py:35
  74.3 2.6 %shard_map.72.keep = f32[4,8,128,128]{3,2,1,0:T(8,128)S(1)} custom-call(s32[5,416]{1,0:T(8,128)S(1)} %get-tuple-element.37.lists, bf16[352,128,128]{2,1,0:T(8,128)(2,1)S(1)} %get-tuple-element.29.values, bf16[8,128,128]{2,1,0:T(8,128)(2,1)S(1)} %get-tuple-element.38.refs_0_, bf16[8,128,128]{2,1,0:T(8,128)(2,1)S(1)} %collective-permute-done.18.refs_1_, ...), custom_call_target="tpu_custom_call" | custom-call | flops 1476395008 | bytes 11534336 | tf_op jit(solution)/shard_map/pallas_call | solution.py:131
  77.0 0.2 shard_map.74
  77.1 1.9 %collective-permute-start.26 = (bf16[4,128,128]{2,1,0:T(8,128)(2,1)S(1)}, bf16[4,128,128]{2,1,0:T(8,128)(2,1)S(1)}, u32[]{:S(2)}, u32[]{:S(2)}) collective-permute-start(bf16[4,128,128]{2,1,0:T(8,128)(2,1)S(1)} %get-tuple-element.49), channel_id=1, source_target_pairs={{0,8},{4,12},{8,0},{12,4},{16,24},{20,28},{24,16},{28,20},{1,9},{5... | collective-permute-start | bytes 393224 | tf_op jit(solution)/shard_map/ppermute | solution.py:35
  79.1 0.2 collective-permute-start.28
  79.2 1.9 %collective-permute-start.25 = (bf16[8,128,128]{2,1,0:T(8,128)(2,1)S(1)}, bf16[8,128,128]{2,1,0:T(8,128)(2,1)S(1)}, u32[]{:S(2)}, u32[]{:S(2)}) collective-permute-start(bf16[8,128,128]{2,1,0:T(8,128)(2,1)S(1)} %get-tuple-element.47), channel_id=1, source_target_pairs={{0,8},{4,12},{8,0},{12,4},{16,24},{20,28},{24,16},{28,20},{1,9},{5... | collective-permute-start | bytes 786440 | tf_op jit(solution)/shard_map/ppermute | solution.py:35
  81.1 2.0 %collective-permute-done.26 = bf16[4,128,128]{2,1,0:T(8,128)(2,1)S(1)} collective-permute-done((bf16[4,128,128]{2,1,0:T(8,128)(2,1)S(1)}, bf16[4,128,128]{2,1,0:T(8,128)(2,1)S(1)}, u32[]{:S(2)}, u32[]{:S(2)}) %collective-permute-start.26) | collective-permute-done | bytes 131104 | tf_op jit(solution)/shard_map/ppermute | solution.py:35
  83.1 1.9 %collective-permute-start.27 = (bf16[4,128,128]{2,1,0:T(8,128)(2,1)S(1)}, bf16[4,128,128]{2,1,0:T(8,128)(2,1)S(1)}, u32[]{:S(2)}, u32[]{:S(2)}) collective-permute-start(bf16[4,128,128]{2,1,0:T(8,128)(2,1)S(1)} %add_convert_fusion.1), channel_id=1, source_target_pairs={{0,16},{4,20},{8,24},{12,28},{16,0},{20,4},{24,8},{28,12},{1,17},{... | collective-permute-start | bytes 393224 | tf_op jit(solution)/shard_map/ppermute | solution.py:35
  85.0 0.9 collective-permute-done.28
  85.9 1.9 %collective-permute-start.29 = (bf16[4,128,128]{2,1,0:T(8,128)(2,1)S(1)}, bf16[4,128,128]{2,1,0:T(8,128)(2,1)S(1)}, u32[]{:S(2)}, u32[]{:S(2)}) collective-permute-start(bf16[4,128,128]{2,1,0:T(8,128)(2,1)S(1)} %add_convert_fusion), channel_id=1, source_target_pairs={{0,16},{4,20},{8,24},{12,28},{16,0},{20,4},{24,8},{28,12},{1,17},{... | collective-permute-start | bytes 393224 | tf_op jit(solution)/shard_map/ppermute | solution.py:35
  87.8 1.4 %collective-permute-start.24 = (bf16[128,128]{1,0:T(8,128)(2,1)S(1)}, bf16[128,128]{1,0:T(8,128)(2,1)S(1)}, u32[]{:S(2)}, u32[]{:S(2)}) collective-permute-start(bf16[128,128]{1,0:T(8,128)(2,1)S(1)} %convert_element_type.46), channel_id=1, source_target_pairs={{0,3},{1,2},{2,1},{3,0},{4,7},{5,6},{6,5},{7,4},{8,11},{9,10},{10,... | collective-permute-start | bytes 98312 | tf_op jit(solution)/shard_map/ppermute | solution.py:35
  89.2 2.8 %collective-permute-start.23 = (bf16[128,128]{1,0:T(8,128)(2,1)S(1)}, bf16[128,128]{1,0:T(8,128)(2,1)S(1)}, u32[]{:S(2)}, u32[]{:S(2)}) collective-permute-start(bf16[128,128]{1,0:T(8,128)(2,1)S(1)} %convert_element_type.46), channel_id=1, source_target_pairs={{0,2},{1,3},{2,0},{3,1},{4,6},{5,7},{6,4},{7,5},{8,10},{9,11},{10,... | collective-permute-start | bytes 98312 | tf_op jit(solution)/shard_map/ppermute | solution.py:35
  92.0 0.6 collective-permute-done.24.refs_3_
  92.6 2.9 %collective-permute-start.22 = (bf16[128,128]{1,0:T(8,128)(2,1)S(1)}, bf16[128,128]{1,0:T(8,128)(2,1)S(1)}, u32[]{:S(2)}, u32[]{:S(2)}) collective-permute-start(bf16[128,128]{1,0:T(8,128)(2,1)S(1)} %convert_element_type.46), channel_id=1, source_target_pairs={{0,1},{1,0},{2,3},{3,2},{4,5},{5,4},{6,7},{7,6},{8,9},{9,8},{10,11... | collective-permute-start | bytes 98312 | tf_op jit(solution)/shard_map/ppermute | solution.py:35
  95.5 1.9 %collective-permute-done.22.refs_1_ = bf16[128,128]{1,0:T(8,128)(2,1)S(1)} collective-permute-done((bf16[128,128]{1,0:T(8,128)(2,1)S(1)}, bf16[128,128]{1,0:T(8,128)(2,1)S(1)}, u32[]{:S(2)}, u32[]{:S(2)}) %collective-permute-start.22) | collective-permute-done | bytes 32800 | tf_op jit(solution)/shard_map/ppermute | solution.py:35
  97.4 5.4 %shard_map.75 = (f32[128,128]{1,0:T(8,128)S(1)}, bf16[8,128,128]{2,1,0:T(8,128)(2,1)}) custom-call(f32[128,128]{1,0:T(8,128)S(1)} %convert_add_fusion.1.refs_0_, bf16[128,128]{1,0:T(8,128)(2,1)S(1)} %collective-permute-done.22.refs_1_, bf16[128,128]{1,0:T(8,128)(2,1)S(1)} %collective-permute-done.23.refs_2_, ...), custom_call_target="tpu_custom_call" | custom-call | tf_op jit(solution)/shard_map/pallas_call | solution.py:332
  102.8 1.2 shard_map.76
  104.1 1.2 collective-permute-done.30
  105.4 2.0 %collective-permute-start.33 = (bf16[128,128]{1,0:T(8,128)(2,1)S(1)}, bf16[128,128]{1,0:T(8,128)(2,1)S(1)}, u32[]{:S(2)}, u32[]{:S(2)}) collective-permute-start(bf16[128,128]{1,0:T(8,128)(2,1)S(1)} %get-tuple-element.56), channel_id=1, source_target_pairs={{0,3},{1,2},{2,1},{3,0},{4,7},{5,6},{6,5},{7,4},{8,11},{9,10},{10,... | collective-permute-start | bytes 98312 | tf_op jit(solution)/shard_map/ppermute | solution.py:35
  107.4 1.6 %collective-permute-start.32 = (bf16[128,128]{1,0:T(8,128)(2,1)S(1)}, bf16[128,128]{1,0:T(8,128)(2,1)S(1)}, u32[]{:S(2)}, u32[]{:S(2)}) collective-permute-start(bf16[128,128]{1,0:T(8,128)(2,1)S(1)} %get-tuple-element.56), channel_id=1, source_target_pairs={{0,2},{1,3},{2,0},{3,1},{4,6},{5,7},{6,4},{7,5},{8,10},{9,11},{10,... | collective-permute-start | bytes 98312 | tf_op jit(solution)/shard_map/ppermute | solution.py:35
  108.9 0.5 collective-permute-start.31
  109.4 1.0 collective-permute-done.33
  110.4 0.9 collective-permute-done.32
  111.3 1.6 %collective-permute-done.31 = bf16[128,128]{1,0:T(8,128)(2,1)S(1)} collective-permute-done((bf16[128,128]{1,0:T(8,128)(2,1)S(1)}, bf16[128,128]{1,0:T(8,128)(2,1)S(1)}, u32[]{:S(2)}, u32[]{:S(2)}) %collective-permute-start.31) | collective-permute-done | bytes 32800 | tf_op jit(solution)/shard_map/ppermute | solution.py:35
  112.9 0.2 collective-permute-start.36
  113.0 1.8 %collective-permute-start.35 = (bf16[128,128]{1,0:T(8,128)(2,1)S(1)}, bf16[128,128]{1,0:T(8,128)(2,1)S(1)}, u32[]{:S(2)}, u32[]{:S(2)}) collective-permute-start(bf16[128,128]{1,0:T(8,128)(2,1)S(1)} %get-tuple-element.54), channel_id=1, source_target_pairs={{0,16},{4,20},{8,24},{12,28},{16,0},{20,4},{24,8},{28,12},{1,17},{... | collective-permute-start | bytes 98312 | tf_op jit(solution)/shard_map/ppermute | solution.py:35
  114.9 2.5 %collective-permute-start.34 = (bf16[128,128]{1,0:T(8,128)(2,1)S(1)}, bf16[128,128]{1,0:T(8,128)(2,1)S(1)}, u32[]{:S(2)}, u32[]{:S(2)}) collective-permute-start(bf16[128,128]{1,0:T(8,128)(2,1)S(1)} %get-tuple-element.54), channel_id=1, source_target_pairs={{0,8},{4,12},{8,0},{12,4},{16,24},{20,28},{24,16},{28,20},{1,9},{5... | collective-permute-start | bytes 98312 | tf_op jit(solution)/shard_map/ppermute | solution.py:35
  117.3 1.3 %collective-permute-done.36.refs_3_ = bf16[128,128]{1,0:T(8,128)(2,1)S(1)} collective-permute-done((bf16[128,128]{1,0:T(8,128)(2,1)S(1)}, bf16[128,128]{1,0:T(8,128)(2,1)S(1)}, u32[]{:S(2)}, u32[]{:S(2)}) %collective-permute-start.36) | collective-permute-done | bytes 32800 | tf_op jit(solution)/shard_map/ppermute | solution.py:35
  118.7 0.6 collective-permute-done.34.refs_1_
  119.2 5.1 %shard_map.77 = bf16[8,128,128]{2,1,0:T(8,128)(2,1)} custom-call(f32[128,128]{1,0:T(8,128)S(1)} %get-tuple-element.55.refs_0_, bf16[128,128]{1,0:T(8,128)(2,1)S(1)} %collective-permute-done.34.refs_1_, bf16[128,128]{1,0:T(8,128)(2,1)S(1)} %collective-permute-done.35.refs_2_, bf16[128,128]{1,0:T(8,128)(2,1)S(1)} %collective-permute-done.36.refs_3_, ...), custom_call_target="tpu_custom_call" | custom-call | tf_op jit(solution)/shard_map/pallas_call | solution.py:332
  (36 shorter events, 0.3 us)
Async XLA Ops:
  0.6 27.1 %copy-start.1 = (bf16[1024,128]{1,0:T(8,128)(2,1)S(1)}, bf16[1024,128]{1,0:T(8,128)(2,1)}, u32[]{:S(2)}) copy-start(bf16[1024,128]{1,0:T(8,128)(2,1)} %param.5) | copy-start | bytes 786436
  0.6 14.3 %collective-permute-start.7 = (bf16[8,128,128]{2,1,0:T(8,128)(2,1)}, bf16[8,128,128]{2,1,0:T(8,128)(2,1)S(1)}, u32[]{:S(2)}, u32[]{:S(2)}) collective-permute-start(bf16[8,128,128]{2,1,0:T(8,128)(2,1)} %bitcast.5), channel_id=1, source_target_pairs={{0,8},{4,12},{8,0},{12,4},{16,24},{20,28},{24,16},{28,20},{1,9},{5... | collective-permute-start | bytes 786440 | tf_op jit(solution)/shard_map/ppermute | solution.py:35
  4.8 8.8 %collective-permute-start = (bf16[4,128,128]{2,1,0:T(8,128)(2,1)S(1)}, bf16[4,128,128]{2,1,0:T(8,128)(2,1)S(1)}, u32[]{:S(2)}, u32[]{:S(2)}) collective-permute-start(bf16[4,128,128]{2,1,0:T(8,128)(2,1)S(1)} %bitcast.10), channel_id=1, source_target_pairs={{0,16},{4,20},{8,24},{12,28},{16,0},{20,4},{24,8},{28,12},{1,17},{... | collective-permute-start | bytes 393224 | tf_op jit(solution)/shard_map/ppermute | solution.py:35
  7.4 11.7 %collective-permute-start.2 = (bf16[4,128,128]{2,1,0:T(8,128)(2,1)S(1)}, bf16[4,128,128]{2,1,0:T(8,128)(2,1)S(1)}, u32[]{:S(2)}, u32[]{:S(2)}) collective-permute-start(bf16[4,128,128]{2,1,0:T(8,128)(2,1)S(1)} %bitcast.9), channel_id=1, source_target_pairs={{0,16},{4,20},{8,24},{12,28},{16,0},{20,4},{24,8},{28,12},{1,17},{... | collective-permute-start | bytes 393224 | tf_op jit(solution)/shard_map/ppermute | solution.py:35
  13.5 5.6 %collective-permute-start.9 = (bf16[4,128,128]{2,1,0:T(8,128)(2,1)S(1)}, bf16[4,128,128]{2,1,0:T(8,128)(2,1)S(1)}, u32[]{:S(2)}, u32[]{:S(2)}) collective-permute-start(bf16[4,128,128]{2,1,0:T(8,128)(2,1)S(1)} %collective-permute-done.refs_4_), channel_id=1, source_target_pairs={{0,4},{4,0},{8,12},{12,8},{16,20},{20,16},{24,28},{28,24},{1,5},{5... | collective-permute-start | bytes 393224 | tf_op jit(solution)/shard_map/ppermute | solution.py:35
  13.5 14.2 %collective-permute-start.6 = (bf16[8,128,128]{2,1,0:T(8,128)(2,1)}, bf16[8,128,128]{2,1,0:T(8,128)(2,1)S(1)}, u32[]{:S(2)}, u32[]{:S(2)}) collective-permute-start(bf16[8,128,128]{2,1,0:T(8,128)(2,1)} %bitcast.6), channel_id=1, source_target_pairs={{0,4},{4,0},{8,12},{12,8},{16,20},{20,16},{24,28},{28,24},{1,5},{5... | collective-permute-start | bytes 786440 | tf_op jit(solution)/shard_map/ppermute | solution.py:35
  14.9 12.8 %collective-permute-start.8 = (bf16[8,128,128]{2,1,0:T(8,128)(2,1)S(1)}, bf16[8,128,128]{2,1,0:T(8,128)(2,1)S(1)}, u32[]{:S(2)}, u32[]{:S(2)}) collective-permute-start(bf16[8,128,128]{2,1,0:T(8,128)(2,1)S(1)} %collective-permute-done.7.refs_2_), channel_id=1, source_target_pairs={{0,4},{4,0},{8,12},{12,8},{16,20},{20,16},{24,28},{28,24},{1,5},{5... | collective-permute-start | bytes 786440 | tf_op jit(solution)/shard_map/ppermute | solution.py:35
  14.9 12.1 %collective-permute-start.1 = (bf16[4,128,128]{2,1,0:T(8,128)(2,1)S(1)}, bf16[4,128,128]{2,1,0:T(8,128)(2,1)S(1)}, u32[]{:S(2)}, u32[]{:S(2)}) collective-permute-start(bf16[4,128,128]{2,1,0:T(8,128)(2,1)S(1)} %collective-permute-done.refs_4_), channel_id=1, source_target_pairs={{0,8},{4,12},{8,0},{12,4},{16,24},{20,28},{24,16},{28,20},{1,9},{5... | collective-permute-start | bytes 393224 | tf_op jit(solution)/shard_map/ppermute | solution.py:35
  19.2 8.4 %collective-permute-start.3 = (bf16[4,128,128]{2,1,0:T(8,128)(2,1)S(1)}, bf16[4,128,128]{2,1,0:T(8,128)(2,1)S(1)}, u32[]{:S(2)}, u32[]{:S(2)}) collective-permute-start(bf16[4,128,128]{2,1,0:T(8,128)(2,1)S(1)} %collective-permute-done.2.refs_5_), channel_id=1, source_target_pairs={{0,8},{4,12},{8,0},{12,4},{16,24},{20,28},{24,16},{28,20},{1,9},{5... | collective-permute-start | bytes 393224 | tf_op jit(solution)/shard_map/ppermute | solution.py:35
  19.2 8.5 %collective-permute-start.10 = (bf16[4,128,128]{2,1,0:T(8,128)(2,1)S(1)}, bf16[4,128,128]{2,1,0:T(8,128)(2,1)S(1)}, u32[]{:S(2)}, u32[]{:S(2)}) collective-permute-start(bf16[4,128,128]{2,1,0:T(8,128)(2,1)S(1)} %collective-permute-done.2.refs_5_), channel_id=1, source_target_pairs={{0,4},{4,0},{8,12},{12,8},{16,20},{20,16},{24,28},{28,24},{1,5},{5... | collective-permute-start | bytes 393224 | tf_op jit(solution)/shard_map/ppermute | solution.py:35
  19.8 4.3 %copy-start = (bf16[1,1,352,128,128]{4,3,2,1,0:T(8,128)(2,1)S(1)}, bf16[1,1,352,128,128]{4,3,2,1,0:T(8,128)(2,1)}, u32[]{:S(2)}) copy-start(bf16[1,1,352,128,128]{4,3,2,1,0:T(8,128)(2,1)} %values.1) | copy-start | bytes 34603012
  24.1 0.7 copy-start.2
  24.8 0.7 copy-start.3
  27.0 3.7 %collective-permute-start.4 = (bf16[4,128,128]{2,1,0:T(8,128)(2,1)S(1)}, bf16[4,128,128]{2,1,0:T(8,128)(2,1)S(1)}, u32[]{:S(2)}, u32[]{:S(2)}) collective-permute-start(bf16[4,128,128]{2,1,0:T(8,128)(2,1)S(1)} %collective-permute-done.1.refs_0_), channel_id=1, source_target_pairs={{0,4},{4,0},{8,12},{12,8},{16,20},{20,16},{24,28},{28,24},{1,5},{5... | collective-permute-start | bytes 393224 | tf_op jit(solution)/shard_map/ppermute | solution.py:35
  27.6 3.2 %collective-permute-start.5 = (bf16[4,128,128]{2,1,0:T(8,128)(2,1)S(1)}, bf16[4,128,128]{2,1,0:T(8,128)(2,1)S(1)}, u32[]{:S(2)}, u32[]{:S(2)}) collective-permute-start(bf16[4,128,128]{2,1,0:T(8,128)(2,1)S(1)} %collective-permute-done.3.refs_1_), channel_id=1, source_target_pairs={{0,4},{4,0},{8,12},{12,8},{16,20},{20,16},{24,28},{28,24},{1,5},{5... | collective-permute-start | bytes 393224 | tf_op jit(solution)/shard_map/ppermute | solution.py:35
  32.7 7.6 %collective-permute-start.11 = (bf16[8,128,128]{2,1,0:T(8,128)(2,1)S(1)}, bf16[8,128,128]{2,1,0:T(8,128)(2,1)S(1)}, u32[]{:S(2)}, u32[]{:S(2)}) collective-permute-start(bf16[8,128,128]{2,1,0:T(8,128)(2,1)S(1)} %get-tuple-element.31), channel_id=1, source_target_pairs={{0,1},{1,0},{2,3},{3,2},{4,5},{5,4},{6,7},{7,6},{8,9},{9,8},{10,11... | collective-permute-start | bytes 786440 | tf_op jit(solution)/shard_map/ppermute | solution.py:35
  34.3 13.7 %collective-permute-start.12 = (bf16[8,128,128]{2,1,0:T(8,128)(2,1)S(1)}, bf16[8,128,128]{2,1,0:T(8,128)(2,1)S(1)}, u32[]{:S(2)}, u32[]{:S(2)}) collective-permute-start(bf16[8,128,128]{2,1,0:T(8,128)(2,1)S(1)} %get-tuple-element.32), channel_id=1, source_target_pairs={{0,2},{1,3},{2,0},{3,1},{4,6},{5,7},{6,4},{7,5},{8,10},{9,11},{10,... | collective-permute-start | bytes 786440 | tf_op jit(solution)/shard_map/ppermute | solution.py:35
  36.3 13.4 %collective-permute-start.13 = (bf16[8,128,128]{2,1,0:T(8,128)(2,1)S(1)}, bf16[8,128,128]{2,1,0:T(8,128)(2,1)S(1)}, u32[]{:S(2)}, u32[]{:S(2)}) collective-permute-start(bf16[8,128,128]{2,1,0:T(8,128)(2,1)S(1)} %get-tuple-element.33), channel_id=1, source_target_pairs={{0,3},{1,2},{2,1},{3,0},{4,7},{5,6},{6,5},{7,4},{8,11},{9,10},{10,... | collective-permute-start | bytes 786440 | tf_op jit(solution)/shard_map/ppermute | solution.py:35
  50.0 1.3 %collective-permute-start.14 = (f32[128,128]{1,0:T(8,128)S(1)}, f32[128,128]{1,0:T(8,128)S(1)}, u32[]{:S(2)}, u32[]{:S(2)}) collective-permute-start(f32[128,128]{1,0:T(8,128)S(1)} %get-tuple-element.34), channel_id=1, source_target_pairs={{0,4},{4,0},{8,12},{12,8},{16,20},{20,16},{24,28},{28,24},{1,5},{5... | collective-permute-start | bytes 196616 | tf_op jit(solution)/shard_map/ppermute | solution.py:35
  51.3 7.1 %collective-permute-start.17 = (bf16[128,128]{1,0:T(8,128)(2,1)S(1)}, bf16[128,128]{1,0:T(8,128)(2,1)S(1)}, u32[]{:S(2)}, u32[]{:S(2)}) collective-permute-start(bf16[128,128]{1,0:T(8,128)(2,1)S(1)} %get-tuple-element.58), channel_id=1, source_target_pairs={{0,24},{4,28},{8,16},{12,20},{16,8},{20,12},{24,0},{28,4},{1,25},{... | collective-permute-start | bytes 98312 | tf_op jit(solution)/shard_map/ppermute | solution.py:35
  55.5 4.8 %collective-permute-start.16 = (bf16[128,128]{1,0:T(8,128)(2,1)S(1)}, bf16[128,128]{1,0:T(8,128)(2,1)S(1)}, u32[]{:S(2)}, u32[]{:S(2)}) collective-permute-start(bf16[128,128]{1,0:T(8,128)(2,1)S(1)} %get-tuple-element.58), channel_id=1, source_target_pairs={{0,16},{4,20},{8,24},{12,28},{16,0},{20,4},{24,8},{28,12},{1,17},{... | collective-permute-start | bytes 98312 | tf_op jit(solution)/shard_map/ppermute | solution.py:35
  55.5 4.8 %collective-permute-start.15 = (bf16[128,128]{1,0:T(8,128)(2,1)S(1)}, bf16[128,128]{1,0:T(8,128)(2,1)S(1)}, u32[]{:S(2)}, u32[]{:S(2)}) collective-permute-start(bf16[128,128]{1,0:T(8,128)(2,1)S(1)} %get-tuple-element.58), channel_id=1, source_target_pairs={{0,8},{4,12},{8,0},{12,4},{16,24},{20,28},{24,16},{28,20},{1,9},{5... | collective-permute-start | bytes 98312 | tf_op jit(solution)/shard_map/ppermute | solution.py:35
  56.1 10.1 %collective-permute-start.20 = (bf16[8,128,128]{2,1,0:T(8,128)(2,1)S(1)}, bf16[8,128,128]{2,1,0:T(8,128)(2,1)S(1)}, u32[]{:S(2)}, u32[]{:S(2)}) collective-permute-start(bf16[8,128,128]{2,1,0:T(8,128)(2,1)S(1)} %get-tuple-element.38.refs_0_), channel_id=1, source_target_pairs={{0,3},{1,2},{2,1},{3,0},{4,7},{5,6},{6,5},{7,4},{8,11},{9,10},{10,... | collective-permute-start | bytes 786440 | tf_op jit(solution)/shard_map/ppermute | solution.py:35
  57.6 12.8 %collective-permute-start.19 = (bf16[8,128,128]{2,1,0:T(8,128)(2,1)S(1)}, bf16[8,128,128]{2,1,0:T(8,128)(2,1)S(1)}, u32[]{:S(2)}, u32[]{:S(2)}) collective-permute-start(bf16[8,128,128]{2,1,0:T(8,128)(2,1)S(1)} %get-tuple-element.38.refs_0_), channel_id=1, source_target_pairs={{0,2},{1,3},{2,0},{3,1},{4,6},{5,7},{6,4},{7,5},{8,10},{9,11},{10,... | collective-permute-start | bytes 786440 | tf_op jit(solution)/shard_map/ppermute | solution.py:35
  58.4 12.0 %collective-permute-start.18 = (bf16[8,128,128]{2,1,0:T(8,128)(2,1)S(1)}, bf16[8,128,128]{2,1,0:T(8,128)(2,1)S(1)}, u32[]{:S(2)}, u32[]{:S(2)}) collective-permute-start(bf16[8,128,128]{2,1,0:T(8,128)(2,1)S(1)} %get-tuple-element.38.refs_0_), channel_id=1, source_target_pairs={{0,1},{1,0},{2,3},{3,2},{4,5},{5,4},{6,7},{7,6},{8,9},{9,8},{10,11... | collective-permute-start | bytes 786440 | tf_op jit(solution)/shard_map/ppermute | solution.py:35
  72.8 4.1 %collective-permute-start.21 = (bf16[4,8,128,128]{3,2,1,0:T(8,128)(2,1)S(1)}, bf16[4,8,128,128]{3,2,1,0:T(8,128)(2,1)S(1)}, u32[]{:S(2)}, u32[]{:S(2)}) collective-permute-start(bf16[4,8,128,128]{3,2,1,0:T(8,128)(2,1)S(1)} %shard_map.73), channel_id=1, source_target_pairs={{0,4},{4,0},{8,12},{12,8},{16,20},{20,16},{24,28},{28,24},{1,5},{5... | collective-permute-start | bytes 3145736 | tf_op jit(solution)/shard_map/ppermute | solution.py:35
  77.1 6.0 %collective-permute-start.26 = (bf16[4,128,128]{2,1,0:T(8,128)(2,1)S(1)}, bf16[4,128,128]{2,1,0:T(8,128)(2,1)S(1)}, u32[]{:S(2)}, u32[]{:S(2)}) collective-permute-start(bf16[4,128,128]{2,1,0:T(8,128)(2,1)S(1)} %get-tuple-element.49), channel_id=1, source_target_pairs={{0,8},{4,12},{8,0},{12,4},{16,24},{20,28},{24,16},{28,20},{1,9},{5... | collective-permute-start | bytes 393224 | tf_op jit(solution)/shard_map/ppermute | solution.py:35
  79.1 6.8 %collective-permute-start.28 = (bf16[4,128,128]{2,1,0:T(8,128)(2,1)S(1)}, bf16[4,128,128]{2,1,0:T(8,128)(2,1)S(1)}, u32[]{:S(2)}, u32[]{:S(2)}) collective-permute-start(bf16[4,128,128]{2,1,0:T(8,128)(2,1)S(1)} %get-tuple-element.51), channel_id=1, source_target_pairs={{0,8},{4,12},{8,0},{12,4},{16,24},{20,28},{24,16},{28,20},{1,9},{5... | collective-permute-start | bytes 393224 | tf_op jit(solution)/shard_map/ppermute | solution.py:35
  79.2 23.6 %collective-permute-start.25 = (bf16[8,128,128]{2,1,0:T(8,128)(2,1)S(1)}, bf16[8,128,128]{2,1,0:T(8,128)(2,1)S(1)}, u32[]{:S(2)}, u32[]{:S(2)}) collective-permute-start(bf16[8,128,128]{2,1,0:T(8,128)(2,1)S(1)} %get-tuple-element.47), channel_id=1, source_target_pairs={{0,8},{4,12},{8,0},{12,4},{16,24},{20,28},{24,16},{28,20},{1,9},{5... | collective-permute-start | bytes 786440 | tf_op jit(solution)/shard_map/ppermute | solution.py:35
  83.1 19.7 %collective-permute-start.27 = (bf16[4,128,128]{2,1,0:T(8,128)(2,1)S(1)}, bf16[4,128,128]{2,1,0:T(8,128)(2,1)S(1)}, u32[]{:S(2)}, u32[]{:S(2)}) collective-permute-start(bf16[4,128,128]{2,1,0:T(8,128)(2,1)S(1)} %add_convert_fusion.1), channel_id=1, source_target_pairs={{0,16},{4,20},{8,24},{12,28},{16,0},{20,4},{24,8},{28,12},{1,17},{... | collective-permute-start | bytes 393224 | tf_op jit(solution)/shard_map/ppermute | solution.py:35
  85.9 16.9 %collective-permute-start.29 = (bf16[4,128,128]{2,1,0:T(8,128)(2,1)S(1)}, bf16[4,128,128]{2,1,0:T(8,128)(2,1)S(1)}, u32[]{:S(2)}, u32[]{:S(2)}) collective-permute-start(bf16[4,128,128]{2,1,0:T(8,128)(2,1)S(1)} %add_convert_fusion), channel_id=1, source_target_pairs={{0,16},{4,20},{8,24},{12,28},{16,0},{20,4},{24,8},{28,12},{1,17},{... | collective-permute-start | bytes 393224 | tf_op jit(solution)/shard_map/ppermute | solution.py:35
  87.8 4.8 %collective-permute-start.24 = (bf16[128,128]{1,0:T(8,128)(2,1)S(1)}, bf16[128,128]{1,0:T(8,128)(2,1)S(1)}, u32[]{:S(2)}, u32[]{:S(2)}) collective-permute-start(bf16[128,128]{1,0:T(8,128)(2,1)S(1)} %convert_element_type.46), channel_id=1, source_target_pairs={{0,3},{1,2},{2,1},{3,0},{4,7},{5,6},{6,5},{7,4},{8,11},{9,10},{10,... | collective-permute-start | bytes 98312 | tf_op jit(solution)/shard_map/ppermute | solution.py:35
  89.2 6.3 %collective-permute-start.23 = (bf16[128,128]{1,0:T(8,128)(2,1)S(1)}, bf16[128,128]{1,0:T(8,128)(2,1)S(1)}, u32[]{:S(2)}, u32[]{:S(2)}) collective-permute-start(bf16[128,128]{1,0:T(8,128)(2,1)S(1)} %convert_element_type.46), channel_id=1, source_target_pairs={{0,2},{1,3},{2,0},{3,1},{4,6},{5,7},{6,4},{7,5},{8,10},{9,11},{10,... | collective-permute-start | bytes 98312 | tf_op jit(solution)/shard_map/ppermute | solution.py:35
  92.6 4.8 %collective-permute-start.22 = (bf16[128,128]{1,0:T(8,128)(2,1)S(1)}, bf16[128,128]{1,0:T(8,128)(2,1)S(1)}, u32[]{:S(2)}, u32[]{:S(2)}) collective-permute-start(bf16[128,128]{1,0:T(8,128)(2,1)S(1)} %convert_element_type.46), channel_id=1, source_target_pairs={{0,1},{1,0},{2,3},{3,2},{4,5},{5,4},{6,7},{7,6},{8,9},{9,8},{10,11... | collective-permute-start | bytes 98312 | tf_op jit(solution)/shard_map/ppermute | solution.py:35
  104.1 1.3 %collective-permute-start.30 = (f32[128,128]{1,0:T(8,128)S(1)}, f32[128,128]{1,0:T(8,128)S(1)}, u32[]{:S(2)}, u32[]{:S(2)}) collective-permute-start(f32[128,128]{1,0:T(8,128)S(1)} %get-tuple-element.52), channel_id=1, source_target_pairs={{0,4},{4,0},{8,12},{12,8},{16,20},{20,16},{24,28},{28,24},{1,5},{5... | collective-permute-start | bytes 196616 | tf_op jit(solution)/shard_map/ppermute | solution.py:35
  105.4 5.0 %collective-permute-start.33 = (bf16[128,128]{1,0:T(8,128)(2,1)S(1)}, bf16[128,128]{1,0:T(8,128)(2,1)S(1)}, u32[]{:S(2)}, u32[]{:S(2)}) collective-permute-start(bf16[128,128]{1,0:T(8,128)(2,1)S(1)} %get-tuple-element.56), channel_id=1, source_target_pairs={{0,3},{1,2},{2,1},{3,0},{4,7},{5,6},{6,5},{7,4},{8,11},{9,10},{10,... | collective-permute-start | bytes 98312 | tf_op jit(solution)/shard_map/ppermute | solution.py:35
  107.4 3.9 %collective-permute-start.32 = (bf16[128,128]{1,0:T(8,128)(2,1)S(1)}, bf16[128,128]{1,0:T(8,128)(2,1)S(1)}, u32[]{:S(2)}, u32[]{:S(2)}) collective-permute-start(bf16[128,128]{1,0:T(8,128)(2,1)S(1)} %get-tuple-element.56), channel_id=1, source_target_pairs={{0,2},{1,3},{2,0},{3,1},{4,6},{5,7},{6,4},{7,5},{8,10},{9,11},{10,... | collective-permute-start | bytes 98312 | tf_op jit(solution)/shard_map/ppermute | solution.py:35
  108.9 3.9 %collective-permute-start.31 = (bf16[128,128]{1,0:T(8,128)(2,1)S(1)}, bf16[128,128]{1,0:T(8,128)(2,1)S(1)}, u32[]{:S(2)}, u32[]{:S(2)}) collective-permute-start(bf16[128,128]{1,0:T(8,128)(2,1)S(1)} %get-tuple-element.56), channel_id=1, source_target_pairs={{0,1},{1,0},{2,3},{3,2},{4,5},{5,4},{6,7},{7,6},{8,9},{9,8},{10,11... | collective-permute-start | bytes 98312 | tf_op jit(solution)/shard_map/ppermute | solution.py:35
  112.9 5.8 %collective-permute-start.36 = (bf16[128,128]{1,0:T(8,128)(2,1)S(1)}, bf16[128,128]{1,0:T(8,128)(2,1)S(1)}, u32[]{:S(2)}, u32[]{:S(2)}) collective-permute-start(bf16[128,128]{1,0:T(8,128)(2,1)S(1)} %get-tuple-element.54), channel_id=1, source_target_pairs={{0,24},{4,28},{8,16},{12,20},{16,8},{20,12},{24,0},{28,4},{1,25},{... | collective-permute-start | bytes 98312 | tf_op jit(solution)/shard_map/ppermute | solution.py:35
  113.0 5.6 %collective-permute-start.35 = (bf16[128,128]{1,0:T(8,128)(2,1)S(1)}, bf16[128,128]{1,0:T(8,128)(2,1)S(1)}, u32[]{:S(2)}, u32[]{:S(2)}) collective-permute-start(bf16[128,128]{1,0:T(8,128)(2,1)S(1)} %get-tuple-element.54), channel_id=1, source_target_pairs={{0,16},{4,20},{8,24},{12,28},{16,0},{20,4},{24,8},{28,12},{1,17},{... | collective-permute-start | bytes 98312 | tf_op jit(solution)/shard_map/ppermute | solution.py:35
  114.9 4.3 %collective-permute-start.34 = (bf16[128,128]{1,0:T(8,128)(2,1)S(1)}, bf16[128,128]{1,0:T(8,128)(2,1)S(1)}, u32[]{:S(2)}, u32[]{:S(2)}) collective-permute-start(bf16[128,128]{1,0:T(8,128)(2,1)S(1)} %get-tuple-element.54), channel_id=1, source_target_pairs={{0,8},{4,12},{8,0},{12,4},{16,24},{20,28},{24,16},{28,20},{1,9},{5... | collective-permute-start | bytes 98312 | tf_op jit(solution)/shard_map/ppermute | solution.py:35
where the time goes:
time: 125 us; the launch traced here: 124 us
  starting transfers between devices  48.2 us (39%)
  waiting for transfers between devices  44.1 us (35%)
  Pallas kernels  23.8 us (19%)
  local copies, waits for them, and re-layouts  6.63 us (5%)
  between operations  1.49 us (1%)
    ppermute x37, starting transfers between devices, swap(): return lax.ppermute(value, axis, [(i, i ^ mask) for i in range(size)])  48.2 us
    ppermute x37, waiting for transfers between devices, swap(): return lax.ppermute(value, axis, [(i, i ^ mask) for i in range(size)])  44.1 us
    pallas_call x5, Pallas kernels, call(): pl.pallas_call(kernel, out_shape=out_shape, in_specs=[VMEM] * len(args),...  12.3 us
    pallas_call x4, Pallas kernels, run_product(): pl.pallas_call(functools.partial(kernel, form, other), out_shape=out_shap...  10 us
    unnamed x8, local copies, waits for them, and re-layouts  5.64 us
  transfers between devices with their start and end apart: 37, of which 20 were waited for; matrix products, arithmetic and copies ran while one was open for 1% of the time, Pallas kernels for 10%

commit v1 on v0

--- a/solution.py
+++ b/solution.py
@@ -451,9 +451,13 @@
         (shape(block, BF16), square), inverse, own, *jax.tree.leaves(came),
     )
     gram = gram + swap(gram, "row", 1)
-    gram = add_parts(exchange(gram, "col", 1))
+    hops = [("col", 1 << b) for b in range((col_size - 1).bit_length())]
+    hops += [("row", 1 << b) for b in range(1, (row_size - 1).bit_length())]
+    for axis, mask in hops[:-1]:
+        gram = add_parts([gram, swap(gram.astype(BF16), axis, mask)])
+    last = [gram, swap(gram.astype(BF16), *hops[-1])]
     right_panel = call(
-        right_factor_kernel, shape(block, BF16), *exchange(gram, "row", 2, 2), right_flipped,
+        right_factor_kernel, shape(block, BF16), *last, right_flipped,
         scratch=[pltpu.VMEM((width, width), F32)],
     )
     return (left_panel.reshape(group_rows, width), right_panel.reshape(group_rows, width))

time: 125 us -> 128 us (1.024)
  waiting for transfers between devices: 44.1 us -> 49.8 us
  starting transfers between devices: 48.2 us -> 46 us
    ppermute x37 -> x35, waiting for transfers between devices: 44.1 us -> 49.8 us  [swap(): return lax.ppermute(value, axis, [(i, i ^ mask) for i in range(size)])]
    ppermute x37 -> x35, starting transfers between devices: 48.2 us -> 46 us  [swap(): return lax.ppermute(value, axis, [(i, i ^ mask) for i in range(size)])]
  transfers between devices with their start and end apart: 37 -> 35, of which waited for: 20 -> 19; matrix products, arithmetic and copies ran while one was open for 1% -> 1% of each run, Pallas kernels for 10% -> 10%
where the time goes in v1:
time: 128 us
  waiting for transfers between devices  49.8 us (39%)
  starting transfers between devices  46 us (36%)
  Pallas kernels  23.8 us (19%)
  local copies, waits for them, and re-layouts  6.63 us (5%)
  between operations  1.49 us (1%)
    ppermute x35, waiting for transfers between devices, swap(): return lax.ppermute(value, axis, [(i, i ^ mask) for i in range(size)])  49.8 us
    ppermute x35, starting transfers between devices, swap(): return lax.ppermute(value, axis, [(i, i ^ mask) for i in range(size)])  46 us
    pallas_call x5, Pallas kernels, call(): pl.pallas_call(kernel, out_shape=out_shape, in_specs=[VMEM] * len(args),...  12.3 us
    pallas_call x4, Pallas kernels, run_product(): pl.pallas_call(functools.partial(kernel, form, other), out_shape=out_shap...  10 us
    unnamed x8, local copies, waits for them, and re-layouts  5.64 us
  transfers between devices with their start and end apart: 35, of which 19 were waited for; matrix products, arithmetic and copies ran while one was open for 1% of the time, Pallas kernels for 10%

profile of v1, /device:TPU:0, one launch (start us, length us, event | category | flops | bytes accessed | tf_op | source)
XLA Modules:
  0.0 127.9 jit_solution(1187172967606347561)
XLA Ops:
  0.6 0.0 copy-start.1
  0.6 3.1 %collective-permute-start.7 = (bf16[8,128,128]{2,1,0:T(8,128)(2,1)}, bf16[8,128,128]{2,1,0:T(8,128)(2,1)S(1)}, u32[]{:S(2)}, u32[]{:S(2)}) collective-permute-start(bf16[8,128,128]{2,1,0:T(8,128)(2,1)} %bitcast.5), channel_id=1, source_target_pairs={{0,8},{4,12},{8,0},{12,4},{16,24},{20,28},{24,16},{28,20},{1,9},{5... | collective-permute-start | bytes 786440 | tf_op jit(solution)/shard_map/ppermute | solution.py:35
  3.8 1.0 fusion.5
  4.8 2.7 %collective-permute-start = (bf16[4,128,128]{2,1,0:T(8,128)(2,1)S(1)}, bf16[4,128,128]{2,1,0:T(8,128)(2,1)S(1)}, u32[]{:S(2)}, u32[]{:S(2)}) collective-permute-start(bf16[4,128,128]{2,1,0:T(8,128)(2,1)S(1)} %bitcast.10), channel_id=1, source_target_pairs={{0,16},{4,20},{8,24},{12,28},{16,0},{20,4},{24,8},{28,12},{1,17},{... | collective-permute-start | bytes 393224 | tf_op jit(solution)/shard_map/ppermute | solution.py:35
  7.4 0.3 collective-permute-start.2
  7.7 5.8 %collective-permute-done.refs_4_ = bf16[4,128,128]{2,1,0:T(8,128)(2,1)S(1)} collective-permute-done((bf16[4,128,128]{2,1,0:T(8,128)(2,1)S(1)}, bf16[4,128,128]{2,1,0:T(8,128)(2,1)S(1)}, u32[]{:S(2)}, u32[]{:S(2)}) %collective-permute-start) | collective-permute-done | bytes 131104 | tf_op jit(solution)/shard_map/ppermute | solution.py:35
  13.5 0.5 collective-permute-start.6
  14.0 0.9 collective-permute-done.7.refs_2_
  14.9 2.8 %collective-permute-start.1 = (bf16[4,128,128]{2,1,0:T(8,128)(2,1)S(1)}, bf16[4,128,128]{2,1,0:T(8,128)(2,1)S(1)}, u32[]{:S(2)}, u32[]{:S(2)}) collective-permute-start(bf16[4,128,128]{2,1,0:T(8,128)(2,1)S(1)} %collective-permute-done.refs_4_), channel_id=1, source_target_pairs={{0,8},{4,12},{8,0},{12,4},{16,24},{20,28},{24,16},{28,20},{1,9},{5... | collective-permute-start | bytes 393224 | tf_op jit(solution)/shard_map/ppermute | solution.py:35
  17.7 1.4 %collective-permute-done.2.refs_5_ = bf16[4,128,128]{2,1,0:T(8,128)(2,1)S(1)} collective-permute-done((bf16[4,128,128]{2,1,0:T(8,128)(2,1)S(1)}, bf16[4,128,128]{2,1,0:T(8,128)(2,1)S(1)}, u32[]{:S(2)}, u32[]{:S(2)}) %collective-permute-start.2) | collective-permute-done | bytes 131104 | tf_op jit(solution)/shard_map/ppermute | solution.py:35
  19.8 4.3 %copy-done = bf16[1,1,352,128,128]{4,3,2,1,0:T(8,128)(2,1)S(1)} copy-done((bf16[1,1,352,128,128]{4,3,2,1,0:T(8,128)(2,1)S(1)}, bf16[1,1,352,128,128]{4,3,2,1,0:T(8,128)(2,1)}, u32[]{:S(2)}) %copy-start) | copy-done | bytes 11534360
  24.1 0.7 copy-done.2
  24.8 0.7 copy-done.3
  25.5 1.5 %shard_map.68 = (s32[5,416]{1,0:T(8,128)S(1)}, s32[5,416]{1,0:T(8,128)S(1)}, bf16[352,128,128]{2,1,0:T(8,128)(2,1)S(1)}) custom-call(s32[1,1]{1,0:T(1,128)S(6)} %copy.7.counts, s32[1,1,352]{2,1,0:T(1,128)S(1)} %copy-done.2, s32[1,1,352]{2,1,0:T(1,128)S(1)} %copy-done.3, bf16[1,1,352,128,128]{4,3,2,1,0:T(8,128)(2,1)S(1)} %copy-done), custom_call_target="tpu_custom_call" | custom-call | tf_op jit(solution)/shard_map/pallas_call | solution.py:397
  27.0 0.6 collective-permute-start.4
  27.6 0.1 collective-permute-start.5
  27.7 3.0 %shard_map.69.refs_4_ = f32[33,128,128]{2,1,0:T(8,128)S(1)} custom-call(s32[5,416]{1,0:T(8,128)S(1)} %get-tuple-element.28.lists, bf16[352,128,128]{2,1,0:T(8,128)(2,1)S(1)} %get-tuple-element.29.values, bf16[8,128,128]{2,1,0:T(8,128)(2,1)S(1)} %bitcast.7, bf16[8,128,128]{2,1,0:T(8,128)(2,1)S(1)} %collective-permute-done.6.refs_1_, ...), custom_call_target="tpu_custom_call" | custom-call | flops 1476395008 | bytes 11534336 | tf_op jit(solution)/shard_map/pallas_call | solution.py:131
  30.8 2.0 %shard_map.70 = (f32[8,128,128]{2,1,0:T(8,128)S(1)}, bf16[8,128,128]{2,1,0:T(8,128)(2,1)S(1)}, bf16[8,128,128]{2,1,0:T(8,128)(2,1)S(1)}, bf16[8,128,128]{2,1,0:T(8,128)(2,1)S(1)}) custom-call(s32[5,416]{1,0:T(8,128)S(1)} %get-tuple-element.28.lists, bf16[352,128,128]{2,1,0:T(8,128)(2,1)S(1)} %get-tuple-element.29.values, ...), custom_call_target="tpu_custom_call" | custom-call | flops 1476395008 | bytes 11534336 | tf_op jit(solution)/shard_map/pallas_call | solution.py:131
  32.7 1.6 %collective-permute-start.11 = (bf16[8,128,128]{2,1,0:T(8,128)(2,1)S(1)}, bf16[8,128,128]{2,1,0:T(8,128)(2,1)S(1)}, u32[]{:S(2)}, u32[]{:S(2)}) collective-permute-start(bf16[8,128,128]{2,1,0:T(8,128)(2,1)S(1)} %get-tuple-element.31), channel_id=1, source_target_pairs={{0,1},{1,0},{2,3},{3,2},{4,5},{5,4},{6,7},{7,6},{8,9},{9,8},{10,11... | collective-permute-start | bytes 786440 | tf_op jit(solution)/shard_map/ppermute | solution.py:35
  34.3 2.0 %collective-permute-start.12 = (bf16[8,128,128]{2,1,0:T(8,128)(2,1)S(1)}, bf16[8,128,128]{2,1,0:T(8,128)(2,1)S(1)}, u32[]{:S(2)}, u32[]{:S(2)}) collective-permute-start(bf16[8,128,128]{2,1,0:T(8,128)(2,1)S(1)} %get-tuple-element.32), channel_id=1, source_target_pairs={{0,2},{1,3},{2,0},{3,1},{4,6},{5,7},{6,4},{7,5},{8,10},{9,11},{10,... | collective-permute-start | bytes 786440 | tf_op jit(solution)/shard_map/ppermute | solution.py:35
  36.3 1.4 %collective-permute-start.13 = (bf16[8,128,128]{2,1,0:T(8,128)(2,1)S(1)}, bf16[8,128,128]{2,1,0:T(8,128)(2,1)S(1)}, u32[]{:S(2)}, u32[]{:S(2)}) collective-permute-start(bf16[8,128,128]{2,1,0:T(8,128)(2,1)S(1)} %get-tuple-element.33), channel_id=1, source_target_pairs={{0,3},{1,2},{2,1},{3,0},{4,7},{5,6},{6,5},{7,4},{8,11},{9,10},{10,... | collective-permute-start | bytes 786440 | tf_op jit(solution)/shard_map/ppermute | solution.py:35
  37.7 2.7 %collective-permute-done.11.refs_0_ = bf16[8,128,128]{2,1,0:T(8,128)(2,1)S(1)} collective-permute-done((bf16[8,128,128]{2,1,0:T(8,128)(2,1)S(1)}, bf16[8,128,128]{2,1,0:T(8,128)(2,1)S(1)}, u32[]{:S(2)}, u32[]{:S(2)}) %collective-permute-start.11) | collective-permute-done | bytes 262176 | tf_op jit(solution)/shard_map/ppermute | solution.py:35
  40.4 7.6 %collective-permute-done.12.refs_1_ = bf16[8,128,128]{2,1,0:T(8,128)(2,1)S(1)} collective-permute-done((bf16[8,128,128]{2,1,0:T(8,128)(2,1)S(1)}, bf16[8,128,128]{2,1,0:T(8,128)(2,1)S(1)}, u32[]{:S(2)}, u32[]{:S(2)}) %collective-permute-start.12) | collective-permute-done | bytes 262176 | tf_op jit(solution)/shard_map/ppermute | solution.py:35
  48.0 1.6 %collective-permute-done.13.refs_2_ = bf16[8,128,128]{2,1,0:T(8,128)(2,1)S(1)} collective-permute-done((bf16[8,128,128]{2,1,0:T(8,128)(2,1)S(1)}, bf16[8,128,128]{2,1,0:T(8,128)(2,1)S(1)}, u32[]{:S(2)}, u32[]{:S(2)}) %collective-permute-start.13) | collective-permute-done | bytes 262176 | tf_op jit(solution)/shard_map/ppermute | solution.py:35
  49.6 0.3 shard_map.71
  50.0 0.1 collective-permute-start.14
  50.0 1.2 collective-permute-done.14
  51.3 4.1 %collective-permute-start.17 = (bf16[128,128]{1,0:T(8,128)(2,1)S(1)}, bf16[128,128]{1,0:T(8,128)(2,1)S(1)}, u32[]{:S(2)}, u32[]{:S(2)}) collective-permute-start(bf16[128,128]{1,0:T(8,128)(2,1)S(1)} %get-tuple-element.58), channel_id=1, source_target_pairs={{0,24},{4,28},{8,16},{12,20},{16,8},{20,12},{24,0},{28,4},{1,25},{... | collective-permute-start | bytes 98312 | tf_op jit(solution)/shard_map/ppermute | solution.py:35
  55.5 0.6 collective-permute-start.15
  56.1 1.5 %collective-permute-start.20 = (bf16[8,128,128]{2,1,0:T(8,128)(2,1)S(1)}, bf16[8,128,128]{2,1,0:T(8,128)(2,1)S(1)}, u32[]{:S(2)}, u32[]{:S(2)}) collective-permute-start(bf16[8,128,128]{2,1,0:T(8,128)(2,1)S(1)} %get-tuple-element.38.refs_0_), channel_id=1, source_target_pairs={{0,3},{1,2},{2,1},{3,0},{4,7},{5,6},{6,5},{7,4},{8,11},{9,10},{10,... | collective-permute-start | bytes 786440 | tf_op jit(solution)/shard_map/ppermute | solution.py:35
  57.6 0.8 collective-permute-start.19
  58.4 1.2 collective-permute-start.18
  59.6 0.7 collective-permute-done.16
  60.3 5.9 %collective-permute-done.20.refs_3_ = bf16[8,128,128]{2,1,0:T(8,128)(2,1)S(1)} collective-permute-done((bf16[8,128,128]{2,1,0:T(8,128)(2,1)S(1)}, bf16[8,128,128]{2,1,0:T(8,128)(2,1)S(1)}, u32[]{:S(2)}, u32[]{:S(2)}) %collective-permute-start.20) | collective-permute-done | bytes 262176 | tf_op jit(solution)/shard_map/ppermute | solution.py:35
  66.2 4.2 %collective-permute-done.19.refs_2_ = bf16[8,128,128]{2,1,0:T(8,128)(2,1)S(1)} collective-permute-done((bf16[8,128,128]{2,1,0:T(8,128)(2,1)S(1)}, bf16[8,128,128]{2,1,0:T(8,128)(2,1)S(1)}, u32[]{:S(2)}, u32[]{:S(2)}) %collective-permute-start.19) | collective-permute-done | bytes 262176 | tf_op jit(solution)/shard_map/ppermute | solution.py:35
  70.4 2.4 %shard_map.73 = bf16[4,8,128,128]{3,2,1,0:T(8,128)(2,1)S(1)} custom-call(s32[5,416]{1,0:T(8,128)S(1)} %get-tuple-element.37.lists, bf16[352,128,128]{2,1,0:T(8,128)(2,1)S(1)} %get-tuple-element.29.values, bf16[8,128,128]{2,1,0:T(8,128)(2,1)S(1)} %get-tuple-element.38.refs_0_, bf16[8,128,128]{2,1,0:T(8,128)(2,1)S(1)} %collective-permute-done.18.refs_1_, ...), custom_call_target="tpu_custom_call" | custom-call | flops 1476395008 | bytes 11534336 | tf_op jit(solution)/shard_map/pallas_call | solution.py:131
  72.8 1.5 %collective-permute-start.21 = (bf16[4,8,128,128]{3,2,1,0:T(8,128)(2,1)S(1)}, bf16[4,8,128,128]{3,2,1,0:T(8,128)(2,1)S(1)}, u32[]{:S(2)}, u32[]{:S(2)}) collective-permute-start(bf16[4,8,128,128]{3,2,1,0:T(8,128)(2,1)S(1)} %shard_map.73), channel_id=1, source_target_pairs={{0,4},{4,0},{8,12},{12,8},{16,20},{20,16},{24,28},{28,24},{1,5},{5... | collective-permute-start | bytes 3145736 | tf_op jit(solution)/shard_map/ppermute | solution.py:35
  74.3 2.6 %shard_map.72.keep = f32[4,8,128,128]{3,2,1,0:T(8,128)S(1)} custom-call(s32[5,416]{1,0:T(8,128)S(1)} %get-tuple-element.37.lists, bf16[352,128,128]{2,1,0:T(8,128)(2,1)S(1)} %get-tuple-element.29.values, bf16[8,128,128]{2,1,0:T(8,128)(2,1)S(1)} %get-tuple-element.38.refs_0_, bf16[8,128,128]{2,1,0:T(8,128)(2,1)S(1)} %collective-permute-done.18.refs_1_, ...), custom_call_target="tpu_custom_call" | custom-call | flops 1476395008 | bytes 11534336 | tf_op jit(solution)/shard_map/pallas_call | solution.py:131
  77.0 0.2 shard_map.74
  77.1 1.9 %collective-permute-start.26 = (bf16[4,128,128]{2,1,0:T(8,128)(2,1)S(1)}, bf16[4,128,128]{2,1,0:T(8,128)(2,1)S(1)}, u32[]{:S(2)}, u32[]{:S(2)}) collective-permute-start(bf16[4,128,128]{2,1,0:T(8,128)(2,1)S(1)} %get-tuple-element.49), channel_id=1, source_target_pairs={{0,8},{4,12},{8,0},{12,4},{16,24},{20,28},{24,16},{28,20},{1,9},{5... | collective-permute-start | bytes 393224 | tf_op jit(solution)/shard_map/ppermute | solution.py:35
  79.1 0.2 collective-permute-start.28
  79.2 1.9 %collective-permute-start.25 = (bf16[8,128,128]{2,1,0:T(8,128)(2,1)S(1)}, bf16[8,128,128]{2,1,0:T(8,128)(2,1)S(1)}, u32[]{:S(2)}, u32[]{:S(2)}) collective-permute-start(bf16[8,128,128]{2,1,0:T(8,128)(2,1)S(1)} %get-tuple-element.47), channel_id=1, source_target_pairs={{0,8},{4,12},{8,0},{12,4},{16,24},{20,28},{24,16},{28,20},{1,9},{5... | collective-permute-start | bytes 786440 | tf_op jit(solution)/shard_map/ppermute | solution.py:35
  81.1 2.0 %collective-permute-done.26 = bf16[4,128,128]{2,1,0:T(8,128)(2,1)S(1)} collective-permute-done((bf16[4,128,128]{2,1,0:T(8,128)(2,1)S(1)}, bf16[4,128,128]{2,1,0:T(8,128)(2,1)S(1)}, u32[]{:S(2)}, u32[]{:S(2)}) %collective-permute-start.26) | collective-permute-done | bytes 131104 | tf_op jit(solution)/shard_map/ppermute | solution.py:35
  83.1 1.9 %collective-permute-start.27 = (bf16[4,128,128]{2,1,0:T(8,128)(2,1)S(1)}, bf16[4,128,128]{2,1,0:T(8,128)(2,1)S(1)}, u32[]{:S(2)}, u32[]{:S(2)}) collective-permute-start(bf16[4,128,128]{2,1,0:T(8,128)(2,1)S(1)} %add_convert_fusion.1), channel_id=1, source_target_pairs={{0,16},{4,20},{8,24},{12,28},{16,0},{20,4},{24,8},{28,12},{1,17},{... | collective-permute-start | bytes 393224 | tf_op jit(solution)/shard_map/ppermute | solution.py:35
  85.0 0.9 collective-permute-done.28
  85.9 1.9 %collective-permute-start.29 = (bf16[4,128,128]{2,1,0:T(8,128)(2,1)S(1)}, bf16[4,128,128]{2,1,0:T(8,128)(2,1)S(1)}, u32[]{:S(2)}, u32[]{:S(2)}) collective-permute-start(bf16[4,128,128]{2,1,0:T(8,128)(2,1)S(1)} %add_convert_fusion), channel_id=1, source_target_pairs={{0,16},{4,20},{8,24},{12,28},{16,0},{20,4},{24,8},{28,12},{1,17},{... | collective-permute-start | bytes 393224 | tf_op jit(solution)/shard_map/ppermute | solution.py:35
  87.8 1.4 %collective-permute-start.24 = (bf16[128,128]{1,0:T(8,128)(2,1)S(1)}, bf16[128,128]{1,0:T(8,128)(2,1)S(1)}, u32[]{:S(2)}, u32[]{:S(2)}) collective-permute-start(bf16[128,128]{1,0:T(8,128)(2,1)S(1)} %convert_element_type.52), channel_id=1, source_target_pairs={{0,3},{1,2},{2,1},{3,0},{4,7},{5,6},{6,5},{7,4},{8,11},{9,10},{10,... | collective-permute-start | bytes 98312 | tf_op jit(solution)/shard_map/ppermute | solution.py:35
  89.2 2.8 %collective-permute-start.23 = (bf16[128,128]{1,0:T(8,128)(2,1)S(1)}, bf16[128,128]{1,0:T(8,128)(2,1)S(1)}, u32[]{:S(2)}, u32[]{:S(2)}) collective-permute-start(bf16[128,128]{1,0:T(8,128)(2,1)S(1)} %convert_element_type.52), channel_id=1, source_target_pairs={{0,2},{1,3},{2,0},{3,1},{4,6},{5,7},{6,4},{7,5},{8,10},{9,11},{10,... | collective-permute-start | bytes 98312 | tf_op jit(solution)/shard_map/ppermute | solution.py:35
  92.0 0.6 collective-permute-done.24.refs_3_
  92.6 2.9 %collective-permute-start.22 = (bf16[128,128]{1,0:T(8,128)(2,1)S(1)}, bf16[128,128]{1,0:T(8,128)(2,1)S(1)}, u32[]{:S(2)}, u32[]{:S(2)}) collective-permute-start(bf16[128,128]{1,0:T(8,128)(2,1)S(1)} %convert_element_type.52), channel_id=1, source_target_pairs={{0,1},{1,0},{2,3},{3,2},{4,5},{5,4},{6,7},{7,6},{8,9},{9,8},{10,11... | collective-permute-start | bytes 98312 | tf_op jit(solution)/shard_map/ppermute | solution.py:35
  95.5 1.9 %collective-permute-done.22.refs_1_ = bf16[128,128]{1,0:T(8,128)(2,1)S(1)} collective-permute-done((bf16[128,128]{1,0:T(8,128)(2,1)S(1)}, bf16[128,128]{1,0:T(8,128)(2,1)S(1)}, u32[]{:S(2)}, u32[]{:S(2)}) %collective-permute-start.22) | collective-permute-done | bytes 32800 | tf_op jit(solution)/shard_map/ppermute | solution.py:35
  97.4 5.4 %shard_map.75 = (f32[128,128]{1,0:T(8,128)S(1)}, bf16[8,128,128]{2,1,0:T(8,128)(2,1)}) custom-call(f32[128,128]{1,0:T(8,128)S(1)} %convert_add_fusion.3.refs_0_, bf16[128,128]{1,0:T(8,128)(2,1)S(1)} %collective-permute-done.22.refs_1_, bf16[128,128]{1,0:T(8,128)(2,1)S(1)} %collective-permute-done.23.refs_2_, ...), custom_call_target="tpu_custom_call" | custom-call | tf_op jit(solution)/shard_map/pallas_call | solution.py:332
  102.8 1.2 shard_map.76
  104.1 0.1 collective-permute-start.30
  104.1 1.2 collective-permute-done.30
  105.4 2.1 %collective-permute-start.31 = (bf16[128,128]{1,0:T(8,128)(2,1)S(1)}, bf16[128,128]{1,0:T(8,128)(2,1)S(1)}, u32[]{:S(2)}, u32[]{:S(2)}) collective-permute-start(bf16[128,128]{1,0:T(8,128)(2,1)S(1)} %get-tuple-element.56), channel_id=1, source_target_pairs={{0,1},{1,0},{2,3},{3,2},{4,5},{5,4},{6,7},{7,6},{8,9},{9,8},{10,11... | collective-permute-start | bytes 98312 | tf_op jit(solution)/shard_map/ppermute | solution.py:35
  107.5 1.9 %collective-permute-done.31 = bf16[128,128]{1,0:T(8,128)(2,1)S(1)} collective-permute-done((bf16[128,128]{1,0:T(8,128)(2,1)S(1)}, bf16[128,128]{1,0:T(8,128)(2,1)S(1)}, u32[]{:S(2)}, u32[]{:S(2)}) %collective-permute-start.31) | collective-permute-done | bytes 32800 | tf_op jit(solution)/shard_map/ppermute | solution.py:35
  109.4 2.5 %collective-permute-start.32 = (bf16[128,128]{1,0:T(8,128)(2,1)S(1)}, bf16[128,128]{1,0:T(8,128)(2,1)S(1)}, u32[]{:S(2)}, u32[]{:S(2)}) collective-permute-start(bf16[128,128]{1,0:T(8,128)(2,1)S(1)} %fusion), channel_id=1, source_target_pairs={{0,2},{1,3},{2,0},{3,1},{4,6},{5,7},{6,4},{7,5},{8,10},{9,11},{10,... | collective-permute-start | bytes 98312 | tf_op jit(solution)/shard_map/ppermute | solution.py:35
  111.9 1.9 %collective-permute-done.32 = bf16[128,128]{1,0:T(8,128)(2,1)S(1)} collective-permute-done((bf16[128,128]{1,0:T(8,128)(2,1)S(1)}, bf16[128,128]{1,0:T(8,128)(2,1)S(1)}, u32[]{:S(2)}, u32[]{:S(2)}) %collective-permute-start.32) | collective-permute-done | bytes 32800 | tf_op jit(solution)/shard_map/ppermute | solution.py:35
  113.8 1.4 %collective-permute-start.33 = (bf16[128,128]{1,0:T(8,128)(2,1)S(1)}, bf16[128,128]{1,0:T(8,128)(2,1)S(1)}, u32[]{:S(2)}, u32[]{:S(2)}) collective-permute-start(bf16[128,128]{1,0:T(8,128)(2,1)S(1)} %fusion.1), channel_id=1, source_target_pairs={{0,8},{4,12},{8,0},{12,4},{16,24},{20,28},{24,16},{28,20},{1,9},{5... | collective-permute-start | bytes 98312 | tf_op jit(solution)/shard_map/ppermute | solution.py:35
  115.3 2.5 %collective-permute-done.33 = bf16[128,128]{1,0:T(8,128)(2,1)S(1)} collective-permute-done((bf16[128,128]{1,0:T(8,128)(2,1)S(1)}, bf16[128,128]{1,0:T(8,128)(2,1)S(1)}, u32[]{:S(2)}, u32[]{:S(2)}) %collective-permute-start.33) | collective-permute-done | bytes 32800 | tf_op jit(solution)/shard_map/ppermute | solution.py:35
  117.9 0.3 collective-permute-start.34
  118.1 4.6 %collective-permute-done.34.refs_1_ = bf16[128,128]{1,0:T(8,128)(2,1)S(1)} collective-permute-done((bf16[128,128]{1,0:T(8,128)(2,1)S(1)}, bf16[128,128]{1,0:T(8,128)(2,1)S(1)}, u32[]{:S(2)}, u32[]{:S(2)}) %collective-permute-start.34) | collective-permute-done | bytes 32800 | tf_op jit(solution)/shard_map/ppermute | solution.py:35
  122.7 5.1 %shard_map.77 = bf16[8,128,128]{2,1,0:T(8,128)(2,1)} custom-call(f32[128,128]{1,0:T(8,128)S(1)} %get-tuple-element.55.refs_0_, bf16[128,128]{1,0:T(8,128)(2,1)S(1)} %collective-permute-done.34.refs_1_, bf16[8,128,128]{2,1,0:T(8,128)(2,1)S(1)} %get-tuple-element.53.refs_2_), custom_call_target="tpu_custom_call" | custom-call | tf_op jit(solution)/shard_map/pallas_call | solution.py:332
  (34 shorter events, 0.2 us)
Async XLA Ops:
  0.6 27.1 %copy-start.1 = (bf16[1024,128]{1,0:T(8,128)(2,1)S(1)}, bf16[1024,128]{1,0:T(8,128)(2,1)}, u32[]{:S(2)}) copy-start(bf16[1024,128]{1,0:T(8,128)(2,1)} %param.5) | copy-start | bytes 786436
  0.6 14.3 %collective-permute-start.7 = (bf16[8,128,128]{2,1,0:T(8,128)(2,1)}, bf16[8,128,128]{2,1,0:T(8,128)(2,1)S(1)}, u32[]{:S(2)}, u32[]{:S(2)}) collective-permute-start(bf16[8,128,128]{2,1,0:T(8,128)(2,1)} %bitcast.5), channel_id=1, source_target_pairs={{0,8},{4,12},{8,0},{12,4},{16,24},{20,28},{24,16},{28,20},{1,9},{5... | collective-permute-start | bytes 786440 | tf_op jit(solution)/shard_map/ppermute | solution.py:35
  4.8 8.8 %collective-permute-start = (bf16[4,128,128]{2,1,0:T(8,128)(2,1)S(1)}, bf16[4,128,128]{2,1,0:T(8,128)(2,1)S(1)}, u32[]{:S(2)}, u32[]{:S(2)}) collective-permute-start(bf16[4,128,128]{2,1,0:T(8,128)(2,1)S(1)} %bitcast.10), channel_id=1, source_target_pairs={{0,16},{4,20},{8,24},{12,28},{16,0},{20,4},{24,8},{28,12},{1,17},{... | collective-permute-start | bytes 393224 | tf_op jit(solution)/shard_map/ppermute | solution.py:35
  7.4 11.7 %collective-permute-start.2 = (bf16[4,128,128]{2,1,0:T(8,128)(2,1)S(1)}, bf16[4,128,128]{2,1,0:T(8,128)(2,1)S(1)}, u32[]{:S(2)}, u32[]{:S(2)}) collective-permute-start(bf16[4,128,128]{2,1,0:T(8,128)(2,1)S(1)} %bitcast.9), channel_id=1, source_target_pairs={{0,16},{4,20},{8,24},{12,28},{16,0},{20,4},{24,8},{28,12},{1,17},{... | collective-permute-start | bytes 393224 | tf_op jit(solution)/shard_map/ppermute | solution.py:35
  13.5 5.6 %collective-permute-start.9 = (bf16[4,128,128]{2,1,0:T(8,128)(2,1)S(1)}, bf16[4,128,128]{2,1,0:T(8,128)(2,1)S(1)}, u32[]{:S(2)}, u32[]{:S(2)}) collective-permute-start(bf16[4,128,128]{2,1,0:T(8,128)(2,1)S(1)} %collective-permute-done.refs_4_), channel_id=1, source_target_pairs={{0,4},{4,0},{8,12},{12,8},{16,20},{20,16},{24,28},{28,24},{1,5},{5... | collective-permute-start | bytes 393224 | tf_op jit(solution)/shard_map/ppermute | solution.py:35
  13.5 14.2 %collective-permute-start.6 = (bf16[8,128,128]{2,1,0:T(8,128)(2,1)}, bf16[8,128,128]{2,1,0:T(8,128)(2,1)S(1)}, u32[]{:S(2)}, u32[]{:S(2)}) collective-permute-start(bf16[8,128,128]{2,1,0:T(8,128)(2,1)} %bitcast.6), channel_id=1, source_target_pairs={{0,4},{4,0},{8,12},{12,8},{16,20},{20,16},{24,28},{28,24},{1,5},{5... | collective-permute-start | bytes 786440 | tf_op jit(solution)/shard_map/ppermute | solution.py:35
  14.9 12.8 %collective-permute-start.8 = (bf16[8,128,128]{2,1,0:T(8,128)(2,1)S(1)}, bf16[8,128,128]{2,1,0:T(8,128)(2,1)S(1)}, u32[]{:S(2)}, u32[]{:S(2)}) collective-permute-start(bf16[8,128,128]{2,1,0:T(8,128)(2,1)S(1)} %collective-permute-done.7.refs_2_), channel_id=1, source_target_pairs={{0,4},{4,0},{8,12},{12,8},{16,20},{20,16},{24,28},{28,24},{1,5},{5... | collective-permute-start | bytes 786440 | tf_op jit(solution)/shard_map/ppermute | solution.py:35
  14.9 12.1 %collective-permute-start.1 = (bf16[4,128,128]{2,1,0:T(8,128)(2,1)S(1)}, bf16[4,128,128]{2,1,0:T(8,128)(2,1)S(1)}, u32[]{:S(2)}, u32[]{:S(2)}) collective-permute-start(bf16[4,128,128]{2,1,0:T(8,128)(2,1)S(1)} %collective-permute-done.refs_4_), channel_id=1, source_target_pairs={{0,8},{4,12},{8,0},{12,4},{16,24},{20,28},{24,16},{28,20},{1,9},{5... | collective-permute-start | bytes 393224 | tf_op jit(solution)/shard_map/ppermute | solution.py:35
  19.2 8.4 %collective-permute-start.3 = (bf16[4,128,128]{2,1,0:T(8,128)(2,1)S(1)}, bf16[4,128,128]{2,1,0:T(8,128)(2,1)S(1)}, u32[]{:S(2)}, u32[]{:S(2)}) collective-permute-start(bf16[4,128,128]{2,1,0:T(8,128)(2,1)S(1)} %collective-permute-done.2.refs_5_), channel_id=1, source_target_pairs={{0,8},{4,12},{8,0},{12,4},{16,24},{20,28},{24,16},{28,20},{1,9},{5... | collective-permute-start | bytes 393224 | tf_op jit(solution)/shard_map/ppermute | solution.py:35
  19.2 8.5 %collective-permute-start.10 = (bf16[4,128,128]{2,1,0:T(8,128)(2,1)S(1)}, bf16[4,128,128]{2,1,0:T(8,128)(2,1)S(1)}, u32[]{:S(2)}, u32[]{:S(2)}) collective-permute-start(bf16[4,128,128]{2,1,0:T(8,128)(2,1)S(1)} %collective-permute-done.2.refs_5_), channel_id=1, source_target_pairs={{0,4},{4,0},{8,12},{12,8},{16,20},{20,16},{24,28},{28,24},{1,5},{5... | collective-permute-start | bytes 393224 | tf_op jit(solution)/shard_map/ppermute | solution.py:35
  19.8 4.3 %copy-start = (bf16[1,1,352,128,128]{4,3,2,1,0:T(8,128)(2,1)S(1)}, bf16[1,1,352,128,128]{4,3,2,1,0:T(8,128)(2,1)}, u32[]{:S(2)}) copy-start(bf16[1,1,352,128,128]{4,3,2,1,0:T(8,128)(2,1)} %values.1) | copy-start | bytes 34603012
  24.1 0.7 copy-start.2
  24.8 0.7 copy-start.3
  27.0 3.7 %collective-permute-start.4 = (bf16[4,128,128]{2,1,0:T(8,128)(2,1)S(1)}, bf16[4,128,128]{2,1,0:T(8,128)(2,1)S(1)}, u32[]{:S(2)}, u32[]{:S(2)}) collective-permute-start(bf16[4,128,128]{2,1,0:T(8,128)(2,1)S(1)} %collective-permute-done.1.refs_0_), channel_id=1, source_target_pairs={{0,4},{4,0},{8,12},{12,8},{16,20},{20,16},{24,28},{28,24},{1,5},{5... | collective-permute-start | bytes 393224 | tf_op jit(solution)/shard_map/ppermute | solution.py:35
  27.6 3.2 %collective-permute-start.5 = (bf16[4,128,128]{2,1,0:T(8,128)(2,1)S(1)}, bf16[4,128,128]{2,1,0:T(8,128)(2,1)S(1)}, u32[]{:S(2)}, u32[]{:S(2)}) collective-permute-start(bf16[4,128,128]{2,1,0:T(8,128)(2,1)S(1)} %collective-permute-done.3.refs_1_), channel_id=1, source_target_pairs={{0,4},{4,0},{8,12},{12,8},{16,20},{20,16},{24,28},{28,24},{1,5},{5... | collective-permute-start | bytes 393224 | tf_op jit(solution)/shard_map/ppermute | solution.py:35
  32.7 7.6 %collective-permute-start.11 = (bf16[8,128,128]{2,1,0:T(8,128)(2,1)S(1)}, bf16[8,128,128]{2,1,0:T(8,128)(2,1)S(1)}, u32[]{:S(2)}, u32[]{:S(2)}) collective-permute-start(bf16[8,128,128]{2,1,0:T(8,128)(2,1)S(1)} %get-tuple-element.31), channel_id=1, source_target_pairs={{0,1},{1,0},{2,3},{3,2},{4,5},{5,4},{6,7},{7,6},{8,9},{9,8},{10,11... | collective-permute-start | bytes 786440 | tf_op jit(solution)/shard_map/ppermute | solution.py:35
  34.3 13.7 %collective-permute-start.12 = (bf16[8,128,128]{2,1,0:T(8,128)(2,1)S(1)}, bf16[8,128,128]{2,1,0:T(8,128)(2,1)S(1)}, u32[]{:S(2)}, u32[]{:S(2)}) collective-permute-start(bf16[8,128,128]{2,1,0:T(8,128)(2,1)S(1)} %get-tuple-element.32), channel_id=1, source_target_pairs={{0,2},{1,3},{2,0},{3,1},{4,6},{5,7},{6,4},{7,5},{8,10},{9,11},{10,... | collective-permute-start | bytes 786440 | tf_op jit(solution)/shard_map/ppermute | solution.py:35
  36.3 13.4 %collective-permute-start.13 = (bf16[8,128,128]{2,1,0:T(8,128)(2,1)S(1)}, bf16[8,128,128]{2,1,0:T(8,128)(2,1)S(1)}, u32[]{:S(2)}, u32[]{:S(2)}) collective-permute-start(bf16[8,128,128]{2,1,0:T(8,128)(2,1)S(1)} %get-tuple-element.33), channel_id=1, source_target_pairs={{0,3},{1,2},{2,1},{3,0},{4,7},{5,6},{6,5},{7,4},{8,11},{9,10},{10,... | collective-permute-start | bytes 786440 | tf_op jit(solution)/shard_map/ppermute | solution.py:35
  50.0 1.3 %collective-permute-start.14 = (f32[128,128]{1,0:T(8,128)S(1)}, f32[128,128]{1,0:T(8,128)S(1)}, u32[]{:S(2)}, u32[]{:S(2)}) collective-permute-start(f32[128,128]{1,0:T(8,128)S(1)} %get-tuple-element.34), channel_id=1, source_target_pairs={{0,4},{4,0},{8,12},{12,8},{16,20},{20,16},{24,28},{28,24},{1,5},{5... | collective-permute-start | bytes 196616 | tf_op jit(solution)/shard_map/ppermute | solution.py:35
  51.3 7.1 %collective-permute-start.17 = (bf16[128,128]{1,0:T(8,128)(2,1)S(1)}, bf16[128,128]{1,0:T(8,128)(2,1)S(1)}, u32[]{:S(2)}, u32[]{:S(2)}) collective-permute-start(bf16[128,128]{1,0:T(8,128)(2,1)S(1)} %get-tuple-element.58), channel_id=1, source_target_pairs={{0,24},{4,28},{8,16},{12,20},{16,8},{20,12},{24,0},{28,4},{1,25},{... | collective-permute-start | bytes 98312 | tf_op jit(solution)/shard_map/ppermute | solution.py:35
  55.5 4.8 %collective-permute-start.16 = (bf16[128,128]{1,0:T(8,128)(2,1)S(1)}, bf16[128,128]{1,0:T(8,128)(2,1)S(1)}, u32[]{:S(2)}, u32[]{:S(2)}) collective-permute-start(bf16[128,128]{1,0:T(8,128)(2,1)S(1)} %get-tuple-element.58), channel_id=1, source_target_pairs={{0,16},{4,20},{8,24},{12,28},{16,0},{20,4},{24,8},{28,12},{1,17},{... | collective-permute-start | bytes 98312 | tf_op jit(solution)/shard_map/ppermute | solution.py:35
  55.5 4.8 %collective-permute-start.15 = (bf16[128,128]{1,0:T(8,128)(2,1)S(1)}, bf16[128,128]{1,0:T(8,128)(2,1)S(1)}, u32[]{:S(2)}, u32[]{:S(2)}) collective-permute-start(bf16[128,128]{1,0:T(8,128)(2,1)S(1)} %get-tuple-element.58), channel_id=1, source_target_pairs={{0,8},{4,12},{8,0},{12,4},{16,24},{20,28},{24,16},{28,20},{1,9},{5... | collective-permute-start | bytes 98312 | tf_op jit(solution)/shard_map/ppermute | solution.py:35
  56.1 10.1 %collective-permute-start.20 = (bf16[8,128,128]{2,1,0:T(8,128)(2,1)S(1)}, bf16[8,128,128]{2,1,0:T(8,128)(2,1)S(1)}, u32[]{:S(2)}, u32[]{:S(2)}) collective-permute-start(bf16[8,128,128]{2,1,0:T(8,128)(2,1)S(1)} %get-tuple-element.38.refs_0_), channel_id=1, source_target_pairs={{0,3},{1,2},{2,1},{3,0},{4,7},{5,6},{6,5},{7,4},{8,11},{9,10},{10,... | collective-permute-start | bytes 786440 | tf_op jit(solution)/shard_map/ppermute | solution.py:35
  57.6 12.8 %collective-permute-start.19 = (bf16[8,128,128]{2,1,0:T(8,128)(2,1)S(1)}, bf16[8,128,128]{2,1,0:T(8,128)(2,1)S(1)}, u32[]{:S(2)}, u32[]{:S(2)}) collective-permute-start(bf16[8,128,128]{2,1,0:T(8,128)(2,1)S(1)} %get-tuple-element.38.refs_0_), channel_id=1, source_target_pairs={{0,2},{1,3},{2,0},{3,1},{4,6},{5,7},{6,4},{7,5},{8,10},{9,11},{10,... | collective-permute-start | bytes 786440 | tf_op jit(solution)/shard_map/ppermute | solution.py:35
  58.4 12.0 %collective-permute-start.18 = (bf16[8,128,128]{2,1,0:T(8,128)(2,1)S(1)}, bf16[8,128,128]{2,1,0:T(8,128)(2,1)S(1)}, u32[]{:S(2)}, u32[]{:S(2)}) collective-permute-start(bf16[8,128,128]{2,1,0:T(8,128)(2,1)S(1)} %get-tuple-element.38.refs_0_), channel_id=1, source_target_pairs={{0,1},{1,0},{2,3},{3,2},{4,5},{5,4},{6,7},{7,6},{8,9},{9,8},{10,11... | collective-permute-start | bytes 786440 | tf_op jit(solution)/shard_map/ppermute | solution.py:35
  72.8 4.1 %collective-permute-start.21 = (bf16[4,8,128,128]{3,2,1,0:T(8,128)(2,1)S(1)}, bf16[4,8,128,128]{3,2,1,0:T(8,128)(2,1)S(1)}, u32[]{:S(2)}, u32[]{:S(2)}) collective-permute-start(bf16[4,8,128,128]{3,2,1,0:T(8,128)(2,1)S(1)} %shard_map.73), channel_id=1, source_target_pairs={{0,4},{4,0},{8,12},{12,8},{16,20},{20,16},{24,28},{28,24},{1,5},{5... | collective-permute-start | bytes 3145736 | tf_op jit(solution)/shard_map/ppermute | solution.py:35
  77.1 6.0 %collective-permute-start.26 = (bf16[4,128,128]{2,1,0:T(8,128)(2,1)S(1)}, bf16[4,128,128]{2,1,0:T(8,128)(2,1)S(1)}, u32[]{:S(2)}, u32[]{:S(2)}) collective-permute-start(bf16[4,128,128]{2,1,0:T(8,128)(2,1)S(1)} %get-tuple-element.49), channel_id=1, source_target_pairs={{0,8},{4,12},{8,0},{12,4},{16,24},{20,28},{24,16},{28,20},{1,9},{5... | collective-permute-start | bytes 393224 | tf_op jit(solution)/shard_map/ppermute | solution.py:35
  79.1 6.8 %collective-permute-start.28 = (bf16[4,128,128]{2,1,0:T(8,128)(2,1)S(1)}, bf16[4,128,128]{2,1,0:T(8,128)(2,1)S(1)}, u32[]{:S(2)}, u32[]{:S(2)}) collective-permute-start(bf16[4,128,128]{2,1,0:T(8,128)(2,1)S(1)} %get-tuple-element.51), channel_id=1, source_target_pairs={{0,8},{4,12},{8,0},{12,4},{16,24},{20,28},{24,16},{28,20},{1,9},{5... | collective-permute-start | bytes 393224 | tf_op jit(solution)/shard_map/ppermute | solution.py:35
  79.2 23.6 %collective-permute-start.25 = (bf16[8,128,128]{2,1,0:T(8,128)(2,1)S(1)}, bf16[8,128,128]{2,1,0:T(8,128)(2,1)S(1)}, u32[]{:S(2)}, u32[]{:S(2)}) collective-permute-start(bf16[8,128,128]{2,1,0:T(8,128)(2,1)S(1)} %get-tuple-element.47), channel_id=1, source_target_pairs={{0,8},{4,12},{8,0},{12,4},{16,24},{20,28},{24,16},{28,20},{1,9},{5... | collective-permute-start | bytes 786440 | tf_op jit(solution)/shard_map/ppermute | solution.py:35
  83.1 19.7 %collective-permute-start.27 = (bf16[4,128,128]{2,1,0:T(8,128)(2,1)S(1)}, bf16[4,128,128]{2,1,0:T(8,128)(2,1)S(1)}, u32[]{:S(2)}, u32[]{:S(2)}) collective-permute-start(bf16[4,128,128]{2,1,0:T(8,128)(2,1)S(1)} %add_convert_fusion.1), channel_id=1, source_target_pairs={{0,16},{4,20},{8,24},{12,28},{16,0},{20,4},{24,8},{28,12},{1,17},{... | collective-permute-start | bytes 393224 | tf_op jit(solution)/shard_map/ppermute | solution.py:35
  85.9 16.9 %collective-permute-start.29 = (bf16[4,128,128]{2,1,0:T(8,128)(2,1)S(1)}, bf16[4,128,128]{2,1,0:T(8,128)(2,1)S(1)}, u32[]{:S(2)}, u32[]{:S(2)}) collective-permute-start(bf16[4,128,128]{2,1,0:T(8,128)(2,1)S(1)} %add_convert_fusion), channel_id=1, source_target_pairs={{0,16},{4,20},{8,24},{12,28},{16,0},{20,4},{24,8},{28,12},{1,17},{... | collective-permute-start | bytes 393224 | tf_op jit(solution)/shard_map/ppermute | solution.py:35
  87.8 4.8 %collective-permute-start.24 = (bf16[128,128]{1,0:T(8,128)(2,1)S(1)}, bf16[128,128]{1,0:T(8,128)(2,1)S(1)}, u32[]{:S(2)}, u32[]{:S(2)}) collective-permute-start(bf16[128,128]{1,0:T(8,128)(2,1)S(1)} %convert_element_type.52), channel_id=1, source_target_pairs={{0,3},{1,2},{2,1},{3,0},{4,7},{5,6},{6,5},{7,4},{8,11},{9,10},{10,... | collective-permute-start | bytes 98312 | tf_op jit(solution)/shard_map/ppermute | solution.py:35
  89.2 6.3 %collective-permute-start.23 = (bf16[128,128]{1,0:T(8,128)(2,1)S(1)}, bf16[128,128]{1,0:T(8,128)(2,1)S(1)}, u32[]{:S(2)}, u32[]{:S(2)}) collective-permute-start(bf16[128,128]{1,0:T(8,128)(2,1)S(1)} %convert_element_type.52), channel_id=1, source_target_pairs={{0,2},{1,3},{2,0},{3,1},{4,6},{5,7},{6,4},{7,5},{8,10},{9,11},{10,... | collective-permute-start | bytes 98312 | tf_op jit(solution)/shard_map/ppermute | solution.py:35
  92.6 4.8 %collective-permute-start.22 = (bf16[128,128]{1,0:T(8,128)(2,1)S(1)}, bf16[128,128]{1,0:T(8,128)(2,1)S(1)}, u32[]{:S(2)}, u32[]{:S(2)}) collective-permute-start(bf16[128,128]{1,0:T(8,128)(2,1)S(1)} %convert_element_type.52), channel_id=1, source_target_pairs={{0,1},{1,0},{2,3},{3,2},{4,5},{5,4},{6,7},{7,6},{8,9},{9,8},{10,11... | collective-permute-start | bytes 98312 | tf_op jit(solution)/shard_map/ppermute | solution.py:35
  104.1 1.3 %collective-permute-start.30 = (f32[128,128]{1,0:T(8,128)S(1)}, f32[128,128]{1,0:T(8,128)S(1)}, u32[]{:S(2)}, u32[]{:S(2)}) collective-permute-start(f32[128,128]{1,0:T(8,128)S(1)} %get-tuple-element.52), channel_id=1, source_target_pairs={{0,4},{4,0},{8,12},{12,8},{16,20},{20,16},{24,28},{28,24},{1,5},{5... | collective-permute-start | bytes 196616 | tf_op jit(solution)/shard_map/ppermute | solution.py:35
  105.4 4.0 %collective-permute-start.31 = (bf16[128,128]{1,0:T(8,128)(2,1)S(1)}, bf16[128,128]{1,0:T(8,128)(2,1)S(1)}, u32[]{:S(2)}, u32[]{:S(2)}) collective-permute-start(bf16[128,128]{1,0:T(8,128)(2,1)S(1)} %get-tuple-element.56), channel_id=1, source_target_pairs={{0,1},{1,0},{2,3},{3,2},{4,5},{5,4},{6,7},{7,6},{8,9},{9,8},{10,11... | collective-permute-start | bytes 98312 | tf_op jit(solution)/shard_map/ppermute | solution.py:35
  109.4 4.4 %collective-permute-start.32 = (bf16[128,128]{1,0:T(8,128)(2,1)S(1)}, bf16[128,128]{1,0:T(8,128)(2,1)S(1)}, u32[]{:S(2)}, u32[]{:S(2)}) collective-permute-start(bf16[128,128]{1,0:T(8,128)(2,1)S(1)} %fusion), channel_id=1, source_target_pairs={{0,2},{1,3},{2,0},{3,1},{4,6},{5,7},{6,4},{7,5},{8,10},{9,11},{10,... | collective-permute-start | bytes 98312 | tf_op jit(solution)/shard_map/ppermute | solution.py:35
  113.8 4.0 %collective-permute-start.33 = (bf16[128,128]{1,0:T(8,128)(2,1)S(1)}, bf16[128,128]{1,0:T(8,128)(2,1)S(1)}, u32[]{:S(2)}, u32[]{:S(2)}) collective-permute-start(bf16[128,128]{1,0:T(8,128)(2,1)S(1)} %fusion.1), channel_id=1, source_target_pairs={{0,8},{4,12},{8,0},{12,4},{16,24},{20,28},{24,16},{28,20},{1,9},{5... | collective-permute-start | bytes 98312 | tf_op jit(solution)/shard_map/ppermute | solution.py:35
  117.9 4.9 %collective-permute-start.34 = (bf16[128,128]{1,0:T(8,128)(2,1)S(1)}, bf16[128,128]{1,0:T(8,128)(2,1)S(1)}, u32[]{:S(2)}, u32[]{:S(2)}) collective-permute-start(bf16[128,128]{1,0:T(8,128)(2,1)S(1)} %get-tuple-element.54), channel_id=1, source_target_pairs={{0,16},{4,20},{8,24},{12,28},{16,0},{20,4},{24,8},{28,12},{1,17},{... | collective-permute-start | bytes 98312 | tf_op jit(solution)/shard_map/ppermute | solution.py:35
